TPU v7x, 32 devices: a whole 2x2x4 slice. The times are simulated.
32 devices in a mesh: band: 4 (over y, core), aperture: 8 (over z, x).
Axes of the slice: x: 2, y: 2, z: 4, core: 2. Of those that a mesh axis runs over, the one named last changes fastest.
Arguments:
- raw_echoes: bfloat16 [1024, 2, 4096], P('aperture', None, 'band'), may hold values from -6 to 6
- pulse_order: int32 [8, 4, 32], P('aperture', 'band'), may hold values from 0 to 31, each once within a row
- matched: float32 [2, 4096], replicated, may hold values from -6 to 6
- offsets: int32 [10, 2, 2, 1], replicated, may hold values from 0 to 16
- fraction: float32 [10, 2, 2], replicated, may hold values from 0 to 0.4
- tilt_angle: float32 [10, 2], replicated, may hold values from -3.140625 to 3.140625
Outputs:
- speckle_image: float32 [1024, 128], P(('band', 'aperture'))
Inputs may be any that keep to these rules, and one draw needn't show every extreme that they name: `pulse_order`: each row of 32 entries names every number below 32 once.
All inputs are finite; a program needn't handle non-finite values.
Results may differ from a plain program's by a relative error of at most 0.0025.
Values may be sent and summed in bfloat16 or wider, within the bound.
No kernel may reach another device: no remote copies, remote signals or barrier semaphores. Data moves between devices by JAX's collectives and lax.ppermute only.
A program may use at most 64 MiB of HBM per device.

v0:
```python
import math

import jax
import jax.numpy as jnp
from jax import lax
from jax.sharding import PartitionSpec as P

FREQ = 4096
R = 128
SHIFT = 8


HIGHEST = lax.Precision.HIGHEST


def swapped(value, axis, apart):
    mask = 2**apart
    pairs = [(source, source ^ mask) for source in range(lax.axis_size(axis))]
    return lax.ppermute(value, axis, pairs)


def range_table(matched_part, freq_start, bin_count):
    freq_count = matched_part.shape[1]
    freq_index = freq_start + jnp.arange(freq_count, dtype=jnp.int32)
    bin_index = jnp.arange(bin_count, dtype=jnp.int32)
    phase_turns = freq_index[:, None] * bin_index[None, :] % FREQ
    phase_angle = phase_turns.astype(jnp.float32) * (2.0 * math.pi / FREQ)
    cosine = jnp.cos(phase_angle)
    sine_part = jnp.sin(phase_angle)
    spec_real = matched_part[0][:, None]
    spec_imag = matched_part[1][:, None]
    norm_scale = 1.0 / math.sqrt(FREQ)
    table_real = (spec_real * cosine - spec_imag * sine_part) * norm_scale
    table_imag = (spec_real * sine_part + spec_imag * cosine) * norm_scale
    upper_rows = jnp.concatenate([table_real, table_imag], axis=1)
    lower_rows = jnp.concatenate([-table_imag, table_real], axis=1)
    return jnp.concatenate([upper_rows, lower_rows], axis=0).astype(jnp.bfloat16)


def interp_kernel(shift_frac):
    in_pos = jnp.arange(128, dtype=jnp.float32)[:, None]
    out_pos = jnp.arange(128, dtype=jnp.float32)[None, :]
    distance = in_pos - out_pos - shift_frac
    tapered = jnp.sinc(distance) * jnp.exp(-((distance / 2.5) ** 2))
    return jnp.where(jnp.abs(distance) <= 4.0, tapered, jnp.zeros_like(tapered))


def merge_pair(first_child, second_child, tree_level, beam_start, offsets, fraction, tilt_angle):
    sub_count = first_child.shape[0]
    row_count = first_child.shape[1]
    range_width = first_child.shape[3]
    halves = []
    for parity in range(2):
        beam_index = (beam_start + 2 * jnp.arange(row_count, dtype=jnp.int32) + parity).astype(
            jnp.float32
        )
        position = 2.0 * (beam_index + 0.5) / 2.0 ** (tree_level + 1) - 1.0
        summed = jnp.zeros(first_child.shape, jnp.float32)
        for child_index, child_image in enumerate((first_child, second_child)):
            padded = jnp.pad(child_image, ((0, 0), (0, 0), (0, 0), (SHIFT, SHIFT)))
            start_cell = 0 + offsets[tree_level, child_index, parity, 0]
            windows = [lax.dynamic_slice_in_dim(padded, start_cell, 128, 3)]
            stacked = jnp.stack(windows, axis=3)
            kernel = interp_kernel(fraction[tree_level, child_index, parity])
            shifted = jnp.einsum("nrckw,wo->nrcko", stacked, kernel, precision=HIGHEST)
            shifted = shifted.reshape(first_child.shape)
            phase_angle = tilt_angle[tree_level, child_index] * position
            cosine = jnp.cos(phase_angle)[None, :, None]
            sine_part = jnp.sin(phase_angle)[None, :, None]
            real_part = shifted[:, :, 0]
            imag_part = shifted[:, :, 1]
            summed = summed + jnp.stack(
                [
                    real_part * cosine - imag_part * sine_part,
                    real_part * sine_part + imag_part * cosine,
                ],
                axis=2,
            )
        halves.append(summed * (1.0 / math.sqrt(2.0)))
    parent = jnp.stack(halves, axis=2)
    return parent.reshape(sub_count, 2 * row_count, 2, range_width)


def box_sum(values):
    row_count = values.shape[1]
    range_width = values.shape[2]
    padded = jnp.pad(values, ((0, 0), (2, 2), (2, 2)))
    across = padded[:, 0:row_count, :]
    for offset_row in range(1, 5):
        across = across + padded[:, offset_row : offset_row + row_count, :]
    summed = across[:, :, 0:range_width]
    for offset_col in range(1, 5):
        summed = summed + across[:, :, offset_col : offset_col + range_width]
    return summed


def speckle(intensity):
    cell_count = box_sum(jnp.ones(intensity.shape, jnp.float32))
    local_mean = box_sum(intensity) / cell_count
    local_square = box_sum(intensity * intensity) / cell_count
    lee_gain = (local_square - local_mean * local_mean) / (
        local_square - 0.75 * local_mean * local_mean + 0.001
    )
    return local_mean + lee_gain * (intensity - local_mean)


def band_sibling(holding, which_half, bit_index):
    half_rows = holding.shape[0] // 2
    own_rows = lax.dynamic_slice_in_dim(holding, which_half * half_rows, half_rows, 0)
    partner_all = swapped(holding, "band", bit_index)
    other_rows = lax.dynamic_slice_in_dim(partner_all, which_half * half_rows, half_rows, 0)
    return (own_rows, other_rows)


def aperture_sibling(holding, which_half, bit_index):
    half_rows = holding.shape[0] // 2
    own_rows = lax.dynamic_slice_in_dim(holding, which_half * half_rows, half_rows, 0)
    partner_all = swapped(holding, "aperture", bit_index)
    other_rows = lax.dynamic_slice_in_dim(partner_all, which_half * half_rows, half_rows, 0)
    return (own_rows, other_rows)


def pair_level(
    holding,
    beam_block,
    which_half,
    tree_level,
    sibling_fn,
    bit_index,
    offsets,
    fraction,
    tilt_angle,
):
    own_rows, other_rows = sibling_fn(holding, which_half, bit_index)
    first_child = jnp.where(which_half == 0, own_rows, other_rows)
    second_child = jnp.where(which_half == 0, other_rows, own_rows)
    beam_block = 2 * beam_block + which_half
    parent = merge_pair(
        first_child[None],
        second_child[None],
        tree_level,
        beam_block * holding.shape[0],
        offsets,
        fraction,
        tilt_angle,
    )
    return (parent[0], beam_block)


def body(raw_echoes, pulse_order, matched, offsets, fraction, tilt_angle):
    pulse_rows = pulse_order.reshape(-1)
    pulse_count = pulse_rows.shape[0]
    freq_local = raw_echoes.shape[2]
    freq_start = lax.axis_index("band") * freq_local
    dft_table = range_table(
        lax.dynamic_slice_in_dim(matched, freq_start, freq_local, 1), freq_start, R
    )
    local_rows = raw_echoes.reshape(raw_echoes.shape[0], 2 * freq_local)
    own_profiles = lax.psum_scatter(
        jnp.dot(local_rows, dft_table, preferred_element_type=jnp.float32),
        "band",
        scatter_dimension=0,
        tiled=True,
    )
    profiles = own_profiles[pulse_rows].reshape(pulse_count, 2, R)
    images = profiles.reshape(pulse_count, 1, 2, R)
    local_levels = pulse_count.bit_length() - 1
    for tree_level in range(local_levels):
        images = merge_pair(
            images[0::2], images[1::2], tree_level, 0, offsets, fraction, tilt_angle
        )
    holding = images[0]
    tree_level = local_levels
    band_bits = lax.axis_size("band").bit_length() - 1
    aperture_bits = lax.axis_size("aperture").bit_length() - 1
    beam_block = jnp.int32(0)
    band_position = lax.axis_index("band")
    for bit_index in range(band_bits):
        which_half = band_position // 2**bit_index % 2
        holding, beam_block = pair_level(
            holding,
            beam_block,
            which_half,
            tree_level,
            band_sibling,
            bit_index,
            offsets,
            fraction,
            tilt_angle,
        )
        tree_level += 1
    aperture_position = lax.axis_index("aperture")
    for bit_index in range(aperture_bits):
        which_half = aperture_position // 2**bit_index % 2
        holding, beam_block = pair_level(
            holding,
            beam_block,
            which_half,
            tree_level,
            aperture_sibling,
            bit_index,
            offsets,
            fraction,
            tilt_angle,
        )
        tree_level += 1
    intensity = holding[:, 0] ** 2 + holding[:, 1] ** 2
    return speckle(intensity[None])[0]


def solution(mesh):
    in_specs = (P("aperture", None, "band"), P("aperture", "band", None), P(), P(), P(), P())
    out_specs = P(("band", "aperture"), None)
    return jax.shard_map(body, mesh=mesh, in_specs=in_specs, out_specs=out_specs, check_vma=False)
```

profile of v0, /device:TPU:0, one launch (start us, length us, event | category | flops | bytes accessed | tf_op | source)
XLA Modules:
  0.0 179.8 jit_solution(11032274424630229571)
XLA Ops:
  6.5 1.2 copy.160
  8.6 2.8 %fusion.15 = (bf16[1024,128]{1,0:T(8,128)(2,1)S(1)}, bf16[1024,128]{1,0:T(8,128)(2,1)S(1)}, bf16[1024,128]{1,0:T(8,128)(2,1)S(1)}) fusion(f32[1024]{0:T(1024)S(1)} %bitcast.670, s32[1024]{0:T(1024)S(1)} %iota_add_fusion, f32[1024]{0:T(1024)S(1)} %bitcast.669), kind=kLoop, calls=%fused_computation.51 | loop fusion | flops 3407872 | bytes 798720 | tf_op jit(solution)/shard_map/convert.5
  78.7 1.4 gather_fusion
  80.1 0.9 convolution_bitcast_fusion.28
  81.8 1.0 convolution_bitcast_fusion.27
  82.8 0.9 convolution_bitcast_fusion.25
  86.8 0.9 fusion.380
  88.4 1.0 fusion.338
  90.5 0.9 fusion.372
  91.5 1.0 fusion.374
  93.9 0.9 fusion.370
  94.8 0.9 fusion.366
  95.7 0.9 fusion.368
  97.8 1.0 convolution_bitcast_fusion.21
  99.6 1.0 convolution_bitcast_fusion.22
  109.7 0.9 convolution_bitcast_fusion.19
  110.6 1.0 convolution_bitcast_fusion.17
  111.6 1.0 convolution_bitcast_fusion.20
  113.8 2.6 %collective-permute-start.1 = (f32[32,2,128]{2,0,1:T(8,128)S(1)}, f32[32,2,128]{2,0,1:T(8,128)S(1)}, u32[]{:S(2)}, u32[]{:S(2)}) collective-permute-start(f32[32,2,128]{2,0,1:T(8,128)S(1)} %bitcast.665), channel_id=1, source_target_pairs={{0,16},{8,24},{16,0},{24,8},{1,17},{9,25},{17,1},{25,9},{2,18},{10... | collective-permute-start | bytes 98312 | tf_op jit(solution)/shard_map/ppermute | solution.py:19
  126.0 0.9 convolution_bitcast_fusion.13
  127.7 0.9 convolution_bitcast_fusion.14
  129.0 1.6 collective-permute-start.2
  139.3 0.9 convolution_bitcast_fusion.11
  140.2 0.9 convolution_bitcast_fusion.9
  143.1 1.6 collective-permute-start.3
  153.7 0.9 convolution_bitcast_fusion.5
  154.6 0.9 convolution_bitcast_fusion.8
  155.5 0.9 convolution_bitcast_fusion.6
  156.8 2.7 %collective-permute-start.4 = (f32[32,2,128]{2,0,1:T(8,128)S(1)}, f32[32,2,128]{2,0,1:T(8,128)S(1)}, u32[]{:S(2)}, u32[]{:S(2)}) collective-permute-start(f32[32,2,128]{2,0,1:T(8,128)S(1)} %bitcast.661), channel_id=1, source_target_pairs={{0,4},{1,5},{2,6},{3,7},{4,0},{5,1},{6,2},{7,3},{8,12},{9,13},{10,... | collective-permute-start | bytes 98312 | tf_op jit(solution)/shard_map/ppermute | solution.py:19
  168.7 0.9 convolution_bitcast_fusion.1
  169.6 0.9 convolution_bitcast_fusion.4
  170.6 1.0 convolution_bitcast_fusion.2
  (189 shorter events, 50.2 us)
Async XLA Ops:
  6.5 72.1 %reduce-scatter.4.cloned.1.call-start = ((), (), s32[]{:S(2)}) async-start(), calls=%async_computation.1 | async-start | bytes 163840 | tf_op jit(solution)/shard_map/reduce_scatter | solution.py:159
  11.3 1.4 copy-start
  11.3 2.7 %copy-start.1 = (f32[10,2,2]{0,2,1:T(2,128)S(1)}, f32[10,2,2]{0,2,1:T(2,128)}, u32[]{:S(2)}) copy-start(f32[10,2,2]{0,2,1:T(2,128)} %param.11) | copy-start | bytes 484
  11.8 3.6 %copy-start.2 = (f32[10,2]{0,1:T(2,128)S(1)}, f32[10,2]{0,1:T(2,128)}, u32[]{:S(2)}) copy-start(f32[10,2]{0,1:T(2,128)} %param.12) | copy-start | bytes 244
  11.8 25.7 %copy-start.3 = (s32[1,1,32]{2,1,0:T(1,128)S(1)}, s32[1,1,32]{2,1,0:T(1,128)}, u32[]{:S(2)}) copy-start(s32[1,1,32]{2,1,0:T(1,128)} %param.8) | copy-start | bytes 388
  100.9 8.7 %collective-permute-start = (f32[32,2,128]{2,0,1:T(8,128)S(1)}, f32[32,2,128]{2,0,1:T(8,128)S(1)}, u32[]{:S(2)}, u32[]{:S(2)}) collective-permute-start(f32[32,2,128]{2,0,1:T(8,128)S(1)} %bitcast.659), channel_id=1, source_target_pairs={{0,8},{8,0},{16,24},{24,16},{1,9},{9,1},{17,25},{25,17},{2,10},{10... | collective-permute-start | bytes 98312 | tf_op jit(solution)/shard_map/ppermute | solution.py:19
  113.8 11.3 %collective-permute-start.1 = (f32[32,2,128]{2,0,1:T(8,128)S(1)}, f32[32,2,128]{2,0,1:T(8,128)S(1)}, u32[]{:S(2)}, u32[]{:S(2)}) collective-permute-start(f32[32,2,128]{2,0,1:T(8,128)S(1)} %bitcast.665), channel_id=1, source_target_pairs={{0,16},{8,24},{16,0},{24,8},{1,17},{9,25},{17,1},{25,9},{2,18},{10... | collective-permute-start | bytes 98312 | tf_op jit(solution)/shard_map/ppermute | solution.py:19
  129.0 10.2 %collective-permute-start.2 = (f32[32,2,128]{2,0,1:T(8,128)S(1)}, f32[32,2,128]{2,0,1:T(8,128)S(1)}, u32[]{:S(2)}, u32[]{:S(2)}) collective-permute-start(f32[32,2,128]{2,0,1:T(8,128)S(1)} %bitcast.663), channel_id=1, source_target_pairs={{0,1},{1,0},{2,3},{3,2},{4,5},{5,4},{6,7},{7,6},{8,9},{9,8},{10,11... | collective-permute-start | bytes 98312 | tf_op jit(solution)/shard_map/ppermute | solution.py:19
  143.1 9.7 %collective-permute-start.3 = (f32[32,2,128]{2,0,1:T(8,128)S(1)}, f32[32,2,128]{2,0,1:T(8,128)S(1)}, u32[]{:S(2)}, u32[]{:S(2)}) collective-permute-start(f32[32,2,128]{2,0,1:T(8,128)S(1)} %bitcast.667), channel_id=1, source_target_pairs={{0,2},{1,3},{2,0},{3,1},{4,6},{5,7},{6,4},{7,5},{8,10},{9,11},{10,... | collective-permute-start | bytes 98312 | tf_op jit(solution)/shard_map/ppermute | solution.py:19
  156.8 11.1 %collective-permute-start.4 = (f32[32,2,128]{2,0,1:T(8,128)S(1)}, f32[32,2,128]{2,0,1:T(8,128)S(1)}, u32[]{:S(2)}, u32[]{:S(2)}) collective-permute-start(f32[32,2,128]{2,0,1:T(8,128)S(1)} %bitcast.661), channel_id=1, source_target_pairs={{0,4},{1,5},{2,6},{3,7},{4,0},{5,1},{6,2},{7,3},{8,12},{9,13},{10,... | collective-permute-start | bytes 98312 | tf_op jit(solution)/shard_map/ppermute | solution.py:19
Sparse Core Ops, SparseCore 0:
  12.7 22.3 reduce-scatter.3
where the time goes:
time: 182 us; the launch traced here: 180 us
  between operations  92.7 us (51%)
  matrix products  36.3 us (20%)
  other arithmetic  30.8 us (17%)
  local copies, waits for them, and re-layouts  10.9 us (6%)
  starting transfers between devices  8.99 us (5%)
    dot_general x40, matrix products, merge_pair(): shifted = jnp.einsum('nrckw,wo->nrcko', stacked, kernel, precision=HIGHEST)  35.9 us
    sin x36, other arithmetic, merge_pair(): sine_part = jnp.sin(phase_angle)[None, :, None]  23.8 us
    ppermute x5, starting transfers between devices, swapped(): return lax.ppermute(value, axis, pairs)  8.99 us
  transfers between devices with their start and end apart: 6, of which 0 were waited for; matrix products, arithmetic and copies ran while one was open for 16% of the time, Pallas kernels for 0%

commit v1 on v0

v1 whole, which is shorter than its diff:
```python
import functools
import math

import jax
import jax.numpy as jnp
from jax import lax
from jax.experimental import pallas as pl
from jax.experimental.pallas import tpu as pltpu
from jax.sharding import PartitionSpec as P

R = 128
SHIFT = 8
LANES = 128
VMEM = pltpu.VMEM
SMEM = pltpu.SMEM


def iota(shape, axis):
    return lax.broadcasted_iota(jnp.int32, shape, axis)


def bit_reversed(value, bits):
    result = value & 0
    for bit in range(bits):
        result = result | (((value >> bit) & 1) << (bits - 1 - bit))
    return result


def halves_of(value):
    high = value.astype(jnp.bfloat16)
    low = (value - high.astype(jnp.float32)).astype(jnp.bfloat16)
    return high, low


def compress_kernel(total_freq, echo_ref, matched_ref, prof_ref, table_ref):
    pulses = echo_ref.shape[0]
    freq = table_ref.shape[1]
    start = lax.axis_index("band") * freq
    scale = 1.0 / math.sqrt(total_freq)
    turn = 2.0 * math.pi / total_freq
    for chunk in range(freq // LANES):
        first = start + chunk * LANES
        lanes = pl.ds(pl.multiple_of(first, LANES), LANES)
        f_index = first + iota((8, LANES), 1)
        angle = ((f_index * iota((8, LANES), 0)) % total_freq).astype(jnp.float32) * turn
        cos_a, sin_a = jnp.cos(angle), jnp.sin(angle)
        angle = ((f_index * 8) % total_freq).astype(jnp.float32) * turn
        cos_w, sin_w = jnp.cos(angle), jnp.sin(angle)
        spec_r = matched_ref[0:1, lanes] * scale
        spec_i = matched_ref[1:2, lanes] * scale
        low_r = spec_r * cos_a - spec_i * sin_a
        low_i = spec_r * sin_a + spec_i * cos_a
        re = jnp.concatenate([low_r, low_r * cos_w - low_i * sin_w], axis=0)
        im = jnp.concatenate([low_i, low_r * sin_w + low_i * cos_w], axis=0)
        two_r = cos_w * cos_w - sin_w * sin_w
        two_i = 2.0 * cos_w * sin_w
        two_r = jnp.concatenate([two_r, two_r], axis=0)
        two_i = jnp.concatenate([two_i, two_i], axis=0)
        here = pl.ds(chunk * LANES, LANES)
        for block in range(R // 16):
            table_ref[pl.ds(block * 16, 16), here] = re.astype(jnp.bfloat16)
            table_ref[pl.ds(R + block * 16, 16), here] = im.astype(jnp.bfloat16)
            if block + 1 < R // 16:
                re, im = re * two_r - im * two_i, re * two_i + im * two_r
    table = table_ref[...]
    dims = (((1,), (1,)), ((), ()))
    from_re = lax.dot_general(
        echo_ref[:, 0:freq], table, dims, preferred_element_type=jnp.float32
    )
    from_im = lax.dot_general(
        echo_ref[:, freq : 2 * freq], table, dims, preferred_element_type=jnp.float32
    )
    prof_ref[0:pulses, :] = from_re[:, 0:R] - from_im[:, R:]
    prof_ref[pulses:, :] = from_re[:, R:] + from_im[:, 0:R]


def build_matrices(first_level, count, offsets_ref, fraction_ref, high_ref, low_ref):
    lane = iota((8, LANES), 1)
    tap = jnp.where(lane < LANES // 2, -lane, LANES - lane).astype(jnp.float32)
    row = iota((8, LANES), 0)
    entries = 4 * count
    base = 4 * first_level
    in_bin, out_bin = iota((R, R), 0), iota((R, R), 1)
    for block in range((entries + 7) // 8):
        shift = jnp.zeros((8, LANES), jnp.float32)
        for sub in range(min(8, entries - block * 8)):
            shift = jnp.where(row == sub, fraction_ref[base + block * 8 + sub], shift)
        dist = tap - shift
        turn = math.pi * dist
        near = jnp.abs(dist) < 1e-12
        sinc = jnp.where(near, 1.0, jnp.sin(turn) / jnp.where(near, 1.0, turn))
        taper = sinc * jnp.exp(-((dist / 2.5) ** 2))
        taper = jnp.where(jnp.abs(dist) <= 4.0, taper, 0.0)
        for sub in range(min(8, entries - block * 8)):
            entry = block * 8 + sub
            moved = offsets_ref[base + entry] - SHIFT
            one = jnp.broadcast_to(taper[sub : sub + 1, :], (8, LANES))
            one = pltpu.roll(one, (LANES - moved) % LANES, 1)
            wide = jnp.broadcast_to(one[0:1, :], (R, LANES))
            wide = pltpu.roll(wide, 0, 1, stride=1, stride_axis=0)
            window = in_bin - moved
            keep = (window >= 0) & (window < R) & (jnp.abs(window - out_bin) <= 4)
            high, low = halves_of(jnp.where(keep, wide, 0.0))
            at = (entry // 2, slice(None), pl.ds((entry % 2) * LANES, LANES))
            high_ref[at] = high
            low_ref[at] = low


def phase_tables(first_level, count, half, inner_bits, tile, tilt_ref):
    bits = half.bit_length() - 1
    lane = iota((1, LANES), 1)
    angle = jnp.zeros((1, LANES), jnp.float32)
    step = jnp.ones((1, LANES), jnp.float32)
    mask = jnp.zeros((1, LANES), jnp.int32)
    tile_start = jnp.zeros((1, LANES), jnp.int32)
    for level in range(count):
        width = inner_bits + level
        here = (lane >> 2) == level
        step = jnp.where(here, 2.0 ** -(first_level + level), step)
        mask = jnp.where(here, 2**width - 1, mask)
        tile_start = jnp.where(here, tile * 2**width, tile_start)
        for child in range(2):
            angle = jnp.where(
                (lane >> 1) == 2 * level + child,
                tilt_ref[2 * (first_level + level) + child],
                angle,
            )
    order = bit_reversed(iota((half, LANES), 0), bits)
    beam = tile_start + (order & mask)
    j_index = (2 * beam + (lane & 1)).astype(jnp.float32)
    phi = angle * ((j_index + 0.5) * step - 1.0)
    norm = 1.0 / math.sqrt(2.0)
    return jnp.cos(phi) * norm, jnp.sin(phi) * norm


def level_step(level, half, source, cos_t, sin_t, high_ref, low_ref):
    products = []
    for child in range(2):
        held = source[pl.ds(child, 2 * half, stride=2), :]
        high, low = halves_of(held)
        m_high, m_low = high_ref[2 * level + child], low_ref[2 * level + child]
        dot = functools.partial(jnp.dot, preferred_element_type=jnp.float32)
        products.append(dot(high, m_high) + (dot(low, m_high) + dot(high, m_low)))
    result = []
    for parity in range(2):
        re = im = None
        for child in range(2):
            entry = 4 * level + 2 * child + parity
            co = cos_t[:, entry : entry + 1]
            si = sin_t[:, entry : entry + 1]
            p_re = products[child][0:half, parity * R : (parity + 1) * R]
            p_im = products[child][half:, parity * R : (parity + 1) * R]
            r_new = p_re * co - p_im * si
            i_new = p_re * si + p_im * co
            re = r_new if re is None else re + r_new
            im = i_new if im is None else im + i_new
        result.append((re, im))
    return result


def local_kernel(count, devices, *refs):
    bands = lax.axis_size("band")
    orders = refs[:bands]
    prof_ref, offsets_ref, fraction_ref, tilt_ref = refs[bands : bands + 4]
    out_ref, high_ref, low_ref, image_ref = refs[bands + 4 :]
    pulses = prof_ref.shape[0] // 2
    half = pulses // 2
    group = pulses // bands
    build_matrices(0, count, offsets_ref, fraction_ref, high_ref, low_ref)
    cos_t, sin_t = phase_tables(0, count, half, 0, 0, tilt_ref)
    me = lax.axis_index("band")
    for apart in range(bands):
        start = pl.multiple_of((me ^ apart) * group, group)
        for pulse in range(group):
            row = start + orders[apart][pulse]
            for part in range(0, 2 * pulses, pulses):
                value = prof_ref[pl.ds(part + row, 1), :]
                image_ref[0, pl.ds(part + start + pulse, 1), :] = value
    kept = pulses // devices
    for level in range(count):
        source, target = image_ref.at[level % 2], image_ref.at[(level + 1) % 2]
        result = level_step(level, half, source, cos_t, sin_t, high_ref, low_ref)
        for parity in range(2):
            for part in range(2):
                value = result[parity][part]
                if level + 1 < count:
                    target[pl.ds(part * pulses + parity * half, half), :] = value
                    continue
                size = min(half, devices)
                for piece in range(half // size):
                    row = parity * half + piece * size
                    begin = (row % devices) * 2 * kept + part * kept + row // devices
                    out_ref[pl.ds(begin, size, stride=2 * kept), :] = value[
                        piece * size : (piece + 1) * size
                    ]


def box(rows):
    total = rows[0]
    for row in rows[1:]:
        total = total + row
    lane = iota(total.shape, 1)
    summed = total
    for off in (1, 2):
        right = pltpu.roll(total, off, 1)
        left = pltpu.roll(total, LANES - off, 1)
        summed = summed + jnp.where(lane >= off, right, 0.0)
        summed = summed + jnp.where(lane < LANES - off, left, 0.0)
    return summed


def near_count(position, size):
    return jnp.minimum(position, 2) + jnp.minimum(size - 1 - position, 2) + 1


def final_kernel(first_level, count, recv_ref, offsets_ref, fraction_ref, tilt_ref, out_ref,
                 high_ref, low_ref, image_ref, pad_ref):
    bands, apertures = lax.axis_size("band"), lax.axis_size("aperture")
    devices = bands * apertures
    rows = out_ref.shape[0]
    half = rows // 2
    kept = rows // apertures
    tile_bits = devices.bit_length() - 1
    inner = kept.bit_length() - 1
    build_matrices(first_level, count, offsets_ref, fraction_ref, high_ref, low_ref)
    place = lax.axis_index("aperture") * bands + lax.axis_index("band")
    tile = bit_reversed(place, tile_bits)
    cos_t, sin_t = phase_tables(first_level, count, half, inner, tile, tilt_ref)
    for part in range(2):
        for beam in range(kept):
            total = None
            for band in range(bands):
                begin = band * 2 * kept + part * kept + beam
                value = recv_ref[pl.ds(begin, apertures, stride=bands * 2 * kept), :]
                total = value if total is None else total + value
            image_ref[0, pl.ds(part * rows + beam * apertures, apertures), :] = total
    for level in range(count):
        source, target = image_ref.at[level % 2], image_ref.at[(level + 1) % 2]
        result = level_step(level, half, source, cos_t, sin_t, high_ref, low_ref)
        for parity in range(2):
            for part in range(2):
                target[pl.ds(part * rows + parity * half, half), :] = result[parity][part]
    last = image_ref.at[count % 2]
    power = last[0:rows, :] ** 2 + last[rows : 2 * rows, :] ** 2
    image_ref[(count + 1) % 2, 0:rows, :] = power
    edge = 8
    for part in range(2):
        pad_ref[part, 0:edge, :] = jnp.zeros((edge, LANES), jnp.float32)
        pad_ref[part, edge + rows :, :] = jnp.zeros((edge, LANES), jnp.float32)
    bits = rows.bit_length() - 1
    for row in range(rows):
        from_row = bit_reversed(row, bits)
        pad_ref[0, edge + row : edge + row + 1, :] = image_ref[
            (count + 1) % 2, from_row : from_row + 1, :
        ]
    power = pad_ref[0, edge : edge + rows, :]
    pad_ref[1, edge : edge + rows, :] = power * power
    sums = [
        box([pad_ref[part, edge + off : edge + off + rows, :] for off in range(-2, 3)])
        for part in range(2)
    ]
    shape = (rows, LANES)
    cells = near_count(iota(shape, 0), rows) * near_count(iota(shape, 1), LANES)
    cells = cells.astype(jnp.float32)
    mean, square = sums[0] / cells, sums[1] / cells
    gain = (square - mean * mean) / (square - 0.75 * mean * mean + 0.001)
    out_ref[...] = mean + gain * (power - mean)


def body(raw_echoes, pulse_order, matched, offsets, fraction, tilt_angle):
    bands, apertures = lax.axis_size("band"), lax.axis_size("aperture")
    devices = bands * apertures
    pulses, _, freq = raw_echoes.shape
    group = pulse_order.shape[-1]
    levels = tilt_angle.shape[0]
    local = pulses.bit_length() - 1
    order = pulse_order.reshape(group)
    orders = [order]
    for apart in range(1, bands):
        orders.append(lax.ppermute(order, "band", [(n, n ^ apart) for n in range(bands)]))
    offsets, fraction = offsets.reshape(-1), fraction.reshape(-1)
    tilt = tilt_angle.reshape(-1)
    vmem, smem = pl.BlockSpec(memory_space=VMEM), pl.BlockSpec(memory_space=SMEM)
    profiles = pl.pallas_call(
        functools.partial(compress_kernel, matched.shape[1]),
        out_shape=jax.ShapeDtypeStruct((2 * pulses, R), jnp.float32),
        in_specs=[vmem, vmem],
        out_specs=vmem,
        scratch_shapes=[VMEM((2 * R, freq), jnp.bfloat16)],
        cost_estimate=pl.CostEstimate(
            flops=8 * pulses * freq * R, bytes_accessed=4 * pulses * freq, transcendentals=0
        ),
        name="compress",
    )(raw_echoes.reshape(pulses, 2 * freq), matched)
    kept = pulses // devices
    sent = pl.pallas_call(
        functools.partial(local_kernel, local, devices),
        out_shape=jax.ShapeDtypeStruct((devices * 2 * kept, R), jnp.float32),
        in_specs=[smem] * bands + [vmem, smem, smem, smem],
        out_specs=vmem,
        scratch_shapes=[
            VMEM((2 * local, R, 2 * R), jnp.bfloat16),
            VMEM((2 * local, R, 2 * R), jnp.bfloat16),
            VMEM((2, 2 * pulses, R), jnp.float32),
        ],
        name="levels",
    )(*orders, profiles, offsets, fraction, tilt)
    received = lax.all_to_all(
        sent.reshape(devices, 2 * kept, R), ("aperture", "band"), 0, 0, tiled=True
    ).reshape(devices * 2 * kept, R)
    rows = kept * apertures
    rest = levels - local
    return pl.pallas_call(
        functools.partial(final_kernel, local, rest),
        out_shape=jax.ShapeDtypeStruct((rows, R), jnp.float32),
        in_specs=[vmem, smem, smem, smem],
        out_specs=vmem,
        scratch_shapes=[
            VMEM((2 * rest, R, 2 * R), jnp.bfloat16),
            VMEM((2 * rest, R, 2 * R), jnp.bfloat16),
            VMEM((2, 2 * rows, R), jnp.float32),
            VMEM((2, rows + 16, R), jnp.float32),
        ],
        name="finish",
    )(received, offsets, fraction, tilt)


def solution(mesh):
    in_specs = (P("aperture", None, "band"), P("aperture", "band", None), P(), P(), P(), P())
    out_specs = P(("band", "aperture"), None)
    return jax.shard_map(body, mesh=mesh, in_specs=in_specs, out_specs=out_specs, check_vma=False)
```

time: 182 us -> 33.2 us (0.18); the launches traced: 180 us -> 32.9 us
  between operations: 92.7 us -> 0.03 us
  matrix products: 36.3 us -> 0 us
  other arithmetic: 30.8 us -> 0 us
  blocking collectives: 0 us -> 14.4 us
  Pallas kernels: 0 us -> 9.32 us
  starting transfers between devices: 8.99 us -> 3.11 us
  local copies, waits for them, and re-layouts: 10.9 us -> 6.04 us
    dot_general x41 -> x0, matrix products: 36.3 us -> none  [the longest x40 35.9 us: merge_pair(): shifted = jnp.einsum('nrckw,wo->nrcko', stacked, kernel, precision=HIGHEST)]
    sin x36 -> x0, other arithmetic: 23.8 us -> none  [merge_pair(): sine_part = jnp.sin(phase_angle)[None, :, None]]
    all_to_all x0 -> x1, blocking collectives: none -> 14.4 us  [body(): lax.all_to_all(sent.reshape(devices, 2 * kept, R), ('aperture', 'band'),...]
    pallas_call x0 -> x3, Pallas kernels: none -> 9.32 us  [the longest x1 4.26 us: body(): pl.pallas_call(functools.partial(local_kernel, local, devices), out_shape...]
    slice x17 -> x0, local copies, waits for them, and re-layouts: 6.99 us -> none  [the longest x3 2.13 us: merge_pair(): start_cell = 0 + offsets[tree_level, child_index, parity, 0]]
    ppermute x5 -> x3, starting transfers between devices: 8.99 us -> 3.11 us  [body(): lax.ppermute(order, 'band', [(n, n ^ apart) for n in range(bands)])]
    another operation x51 -> x0, other arithmetic: 5.76 us -> none  [the longest x41 2.96 us: merge_pair(): jnp.stack([real_part * cosine - imag_part * sine_part, real_part * sine_p...]
    unnamed x14 -> x18, local copies, waits for them, and re-layouts: 1.95 us -> 4.05 us
  transfers between devices with their start and end apart: 6 -> 3, of which waited for: 0 -> 0; matrix products, arithmetic and copies ran while one was open for 16% -> 13% of each run, Pallas kernels for 0% -> 7%
where the time goes in v1:
time: 33.2 us; the launch traced here: 32.9 us
  blocking collectives  14.4 us (43%)
  Pallas kernels  9.32 us (28%)
  local copies, waits for them, and re-layouts  6.04 us (18%)
  starting transfers between devices  3.11 us (9%)
    all_to_all x1, blocking collectives, body(): lax.all_to_all(sent.reshape(devices, 2 * kept, R), ('aperture', 'band'),...  14.4 us
    pallas_call x1, Pallas kernels, body(): pl.pallas_call(functools.partial(local_kernel, local, devices), out_shape...  4.26 us
    unnamed x18, local copies, waits for them, and re-layouts  4.05 us
    ppermute x3, starting transfers between devices, body(): lax.ppermute(order, 'band', [(n, n ^ apart) for n in range(bands)])  3.11 us
    pallas_call x1, Pallas kernels, body(): pl.pallas_call(functools.partial(final_kernel, local, rest), out_shape=ja...  2.65 us
    pallas_call x1, Pallas kernels, body(): pl.pallas_call(functools.partial(compress_kernel, matched.shape[1]), out_...  2.42 us
    reshape x2, local copies, waits for them, and re-layouts, body(): offsets, fraction = (offsets.reshape(-1), fraction.reshape(-1))  1.31 us
    reshape x1, local copies, waits for them, and re-layouts, body(): tilt = tilt_angle.reshape(-1)  0.68 us
  transfers between devices with their start and end apart: 3, of which 0 were waited for; matrix products, arithmetic and copies ran while one was open for 13% of the time, Pallas kernels for 7%

profile of v1, /device:TPU:0, one launch (start us, length us, event | category | flops | bytes accessed | tf_op | source)
XLA Modules:
  0.0 32.9 jit_solution(6044847915782081108)
XLA Ops:
  0.0 0.0 copy-start.3
  0.0 0.7 %copy-done.3 = s32[1,1,32]{2,1,0:T(1,128)S(1)} copy-done((s32[1,1,32]{2,1,0:T(1,128)S(1)}, s32[1,1,32]{2,1,0:T(1,128)}, u32[]{:S(2)}) %copy-start.3) | copy-done | bytes 152
  0.7 0.5 %collective-permute-start = (s32[32]{0:T(128)S(1)}, s32[32]{0:T(128)S(1)}, u32[]{:S(2)}, u32[]{:S(2)}) collective-permute-start(s32[32]{0:T(128)S(1)} %bitcast.12), channel_id=1, source_target_pairs={{0,8},{8,0},{16,24},{24,16},{1,9},{9,1},{17,25},{25,17},{2,10},{10... | collective-permute-start | bytes 392 | tf_op jit(solution)/shard_map/ppermute | solution.py:280
  1.1 2.5 %collective-permute-start.1 = (s32[32]{0:T(128)S(1)}, s32[32]{0:T(128)S(1)}, u32[]{:S(2)}, u32[]{:S(2)}) collective-permute-start(s32[32]{0:T(128)S(1)} %bitcast.13), channel_id=1, source_target_pairs={{0,16},{8,24},{16,0},{24,8},{1,17},{9,25},{17,1},{25,9},{2,18},{10... | collective-permute-start | bytes 392 | tf_op jit(solution)/shard_map/ppermute | solution.py:280
  3.7 0.1 collective-permute-start.2
  3.8 0.0 copy-start
  3.8 2.0 %copy.13 = bf16[16,8,2,1024]{3,1,2,0:T(8,128)(2,1)} copy(bf16[16,8,2,1024]{3,2,1,0:T(2,128)(2,1)} %bitcast.8) | data formatting | bytes 1048576
  5.7 0.0 copy-done
  5.8 0.1 copy.10
  5.9 0.0 copy-start.1
  5.9 0.6 %reshape.23.refs_5_.offsets_ref = s32[40]{0:T(128)} reshape(s32[10,2,2,1]{2,1,0,3:T(2,128)S(1)} %copy.10) | data formatting | bytes 320 | tf_op jit(solution)/shard_map/reshape | solution.py:281
  6.5 0.0 copy-done.1
  6.5 0.1 copy.11
  6.6 0.7 %reshape.24.refs_6_.fraction_ref = f32[40]{0:T(128)} reshape(f32[10,2,2]{2,1,0:T(2,128)S(1)} %copy.11) | data formatting | bytes 320 | tf_op jit(solution)/shard_map/reshape | solution.py:281
  7.3 0.0 copy-start.2
  7.3 2.4 %compress.1.refs_4_ = f32[256,128]{1,0:T(8,128)} custom-call(bf16[128,2048]{1,0:T(8,128)(2,1)} %bitcast.7, f32[2,4096]{1,0:T(2,128)} %matched_ref.1), custom_call_target="tpu_custom_call" | custom-call | flops 134217728 | bytes 524288 | tf_op jit(solution)/shard_map/compress/pallas_call | solution.py:284
  9.7 0.0 copy-done.2
  9.7 0.1 copy.12
  9.8 0.7 %reshape.25.refs_7_.tilt_ref = f32[20]{0:T(128)} reshape(f32[10,2]{1,0:T(8,128)S(1)} %copy.12) | data formatting | bytes 160 | tf_op jit(solution)/shard_map/reshape | solution.py:282
  10.5 0.0 collective-permute-done.refs_1_
  10.5 0.0 copy-start.4
  10.5 0.0 collective-permute-done.1.refs_2_
  10.5 0.0 copy-start.5
  10.5 0.0 collective-permute-done.2.refs_3_
  10.5 0.5 %copy-done.4 = s32[32]{0:T(128)} copy-done((s32[32]{0:T(128)}, s32[32]{0:T(128)S(1)}, u32[]{:S(2)}) %copy-start.4) | copy-done | bytes 152
  11.0 0.0 copy-done.5
  11.0 0.0 copy-start.6
  11.0 0.6 %copy-done.6 = s32[32]{0:T(128)} copy-done((s32[32]{0:T(128)}, s32[32]{0:T(128)S(1)}, u32[]{:S(2)}) %copy-start.6) | copy-done | bytes 152
  11.6 4.3 %levels.1 = f32[256,128]{1,0:T(8,128)} custom-call(s32[32]{0:T(128)} %bitcast.11, s32[32]{0:T(128)} %copy-done.4, s32[32]{0:T(128)} %copy-done.5, s32[32]{0:T(128)} %copy-done.6, f32[256,128]{1,0:T(8,128)} %compress.1.refs_4_, s32[40]{0:T(128)} %reshape.23.refs_5_.offsets_ref, f32[40]{0:T(128)} %reshape.24.refs_6_.fraction_ref, f32[20]{0:T(128)} %reshape.25.refs_7_.tilt_ref), custom_call_target="tpu_custom_call" | custom-call | tf_op jit(solution)/shard_map/levels/pallas_call | solution.py:296
  15.9 14.4 %all_to_all.5 = f32[32,8,128]{2,1,0:T(8,128)} all-to-all(f32[32,8,128]{2,1,0:T(8,128)} %bitcast.9), channel_id=1, replica_groups=mesh['band'=4,'aperture'=8] {'aperture','band'}, dimensions={0} | all-to-all | bytes 262144 | tf_op jit(solution)/shard_map/all_to_all | solution.py:308
  30.3 2.6 %finish.1 = f32[32,128]{1,0:T(8,128)} custom-call(f32[256,128]{1,0:T(8,128)} %bitcast.10, s32[40]{0:T(128)} %reshape.23.refs_5_.offsets_ref, f32[40]{0:T(128)} %reshape.24.refs_6_.fraction_ref, f32[20]{0:T(128)} %reshape.25.refs_7_.tilt_ref), custom_call_target="tpu_custom_call" | custom-call | tf_op jit(solution)/shard_map/finish/pallas_call | solution.py:313
Async XLA Ops:
  0.0 0.7 %copy-start.3 = (s32[1,1,32]{2,1,0:T(1,128)S(1)}, s32[1,1,32]{2,1,0:T(1,128)}, u32[]{:S(2)}) copy-start(s32[1,1,32]{2,1,0:T(1,128)} %param.7) | copy-start | bytes 388
  0.7 9.8 %collective-permute-start = (s32[32]{0:T(128)S(1)}, s32[32]{0:T(128)S(1)}, u32[]{:S(2)}, u32[]{:S(2)}) collective-permute-start(s32[32]{0:T(128)S(1)} %bitcast.12), channel_id=1, source_target_pairs={{0,8},{8,0},{16,24},{24,16},{1,9},{9,1},{17,25},{25,17},{2,10},{10... | collective-permute-start | bytes 392 | tf_op jit(solution)/shard_map/ppermute | solution.py:280
  1.1 9.4 %collective-permute-start.1 = (s32[32]{0:T(128)S(1)}, s32[32]{0:T(128)S(1)}, u32[]{:S(2)}, u32[]{:S(2)}) collective-permute-start(s32[32]{0:T(128)S(1)} %bitcast.13), channel_id=1, source_target_pairs={{0,16},{8,24},{16,0},{24,8},{1,17},{9,25},{17,1},{25,9},{2,18},{10... | collective-permute-start | bytes 392 | tf_op jit(solution)/shard_map/ppermute | solution.py:280
  3.7 6.9 %collective-permute-start.2 = (s32[32]{0:T(128)S(1)}, s32[32]{0:T(128)S(1)}, u32[]{:S(2)}, u32[]{:S(2)}) collective-permute-start(s32[32]{0:T(128)S(1)} %bitcast.14), channel_id=1, source_target_pairs={{0,24},{8,16},{16,8},{24,0},{1,25},{9,17},{17,9},{25,1},{2,26},{10... | collective-permute-start | bytes 392 | tf_op jit(solution)/shard_map/ppermute | solution.py:280
  3.8 2.0 %copy-start = (s32[10,2,2,1]{0,3,2,1:T(1,128)S(1)}, s32[10,2,2,1]{0,3,2,1:T(1,128)}, u32[]{:S(2)}) copy-start(s32[10,2,2,1]{0,3,2,1:T(1,128)} %param.9) | copy-start | bytes 484
  5.9 0.7 %copy-start.1 = (f32[10,2,2]{0,2,1:T(2,128)S(1)}, f32[10,2,2]{0,2,1:T(2,128)}, u32[]{:S(2)}) copy-start(f32[10,2,2]{0,2,1:T(2,128)} %param.10) | copy-start | bytes 484
  7.3 2.4 %copy-start.2 = (f32[10,2]{0,1:T(2,128)S(1)}, f32[10,2]{0,1:T(2,128)}, u32[]{:S(2)}) copy-start(f32[10,2]{0,1:T(2,128)} %param.11) | copy-start | bytes 244
  10.5 0.5 %copy-start.4 = (s32[32]{0:T(128)}, s32[32]{0:T(128)S(1)}, u32[]{:S(2)}) copy-start(s32[32]{0:T(128)S(1)} %collective-permute-done.refs_1_) | copy-start | bytes 388
  10.5 0.5 %copy-start.5 = (s32[32]{0:T(128)}, s32[32]{0:T(128)S(1)}, u32[]{:S(2)}) copy-start(s32[32]{0:T(128)S(1)} %collective-permute-done.1.refs_2_) | copy-start | bytes 388
  11.0 0.6 %copy-start.6 = (s32[32]{0:T(128)}, s32[32]{0:T(128)S(1)}, u32[]{:S(2)}) copy-start(s32[32]{0:T(128)S(1)} %collective-permute-done.2.refs_3_) | copy-start | bytes 388

commit v2 on v1

--- a/solution.py
+++ b/solution.py
@@ -32,10 +32,8 @@
     return high, low
 
 
-def compress_kernel(total_freq, echo_ref, matched_ref, prof_ref, table_ref):
-    pulses = echo_ref.shape[0]
+def make_table(total_freq, start, matched_ref, table_ref):
     freq = table_ref.shape[1]
-    start = lax.axis_index("band") * freq
     scale = 1.0 / math.sqrt(total_freq)
     turn = 2.0 * math.pi / total_freq
     for chunk in range(freq // LANES):
@@ -62,51 +60,46 @@
             table_ref[pl.ds(R + block * 16, 16), here] = im.astype(jnp.bfloat16)
             if block + 1 < R // 16:
                 re, im = re * two_r - im * two_i, re * two_i + im * two_r
-    table = table_ref[...]
-    dims = (((1,), (1,)), ((), ()))
-    from_re = lax.dot_general(
-        echo_ref[:, 0:freq], table, dims, preferred_element_type=jnp.float32
-    )
-    from_im = lax.dot_general(
-        echo_ref[:, freq : 2 * freq], table, dims, preferred_element_type=jnp.float32
-    )
-    prof_ref[0:pulses, :] = from_re[:, 0:R] - from_im[:, R:]
-    prof_ref[pulses:, :] = from_re[:, R:] + from_im[:, 0:R]
-
-
-def build_matrices(first_level, count, offsets_ref, fraction_ref, high_ref, low_ref):
+
+
+def build_matrices(levels, offsets_ref, fraction_ref, high_ref, low_ref):
     lane = iota((8, LANES), 1)
     tap = jnp.where(lane < LANES // 2, -lane, LANES - lane).astype(jnp.float32)
     row = iota((8, LANES), 0)
-    entries = 4 * count
-    base = 4 * first_level
-    in_bin, out_bin = iota((R, R), 0), iota((R, R), 1)
-    for block in range((entries + 7) // 8):
+    entries = [(n, c, p) for n in range(levels) for c in range(2) for p in range(2)]
+    edge = 2 * SHIFT
+    out_bin, in_bin = iota((edge, R), 1), iota((edge, R), 0)
+    for block in range(0, len(entries), 8):
+        here = entries[block : block + 8]
         shift = jnp.zeros((8, LANES), jnp.float32)
-        for sub in range(min(8, entries - block * 8)):
-            shift = jnp.where(row == sub, fraction_ref[base + block * 8 + sub], shift)
+        for sub, (level, child, parity) in enumerate(here):
+            shift = jnp.where(row == sub, fraction_ref[child, parity, level], shift)
         dist = tap - shift
         turn = math.pi * dist
         near = jnp.abs(dist) < 1e-12
         sinc = jnp.where(near, 1.0, jnp.sin(turn) / jnp.where(near, 1.0, turn))
         taper = sinc * jnp.exp(-((dist / 2.5) ** 2))
         taper = jnp.where(jnp.abs(dist) <= 4.0, taper, 0.0)
-        for sub in range(min(8, entries - block * 8)):
-            entry = block * 8 + sub
-            moved = offsets_ref[base + entry] - SHIFT
+        for sub, (level, child, parity) in enumerate(here):
+            moved = offsets_ref[child, parity, 0, level] - SHIFT
             one = jnp.broadcast_to(taper[sub : sub + 1, :], (8, LANES))
             one = pltpu.roll(one, (LANES - moved) % LANES, 1)
             wide = jnp.broadcast_to(one[0:1, :], (R, LANES))
             wide = pltpu.roll(wide, 0, 1, stride=1, stride_axis=0)
             window = in_bin - moved
-            keep = (window >= 0) & (window < R) & (jnp.abs(window - out_bin) <= 4)
-            high, low = halves_of(jnp.where(keep, wide, 0.0))
-            at = (entry // 2, slice(None), pl.ds((entry % 2) * LANES, LANES))
+            keep = (window >= 0) & (jnp.abs(window - out_bin) <= 4)
+            top = jnp.where(keep, wide[0:edge], 0.0)
+            window = window + (R - edge)
+            keep = (window < R) & (jnp.abs(window - out_bin) <= 4)
+            bottom = jnp.where(keep, wide[R - edge :], 0.0)
+            wide = jnp.concatenate([top, wide[edge : R - edge], bottom], axis=0)
+            high, low = halves_of(wide)
+            at = (2 * level + child, slice(None), pl.ds(parity * LANES, LANES))
             high_ref[at] = high
             low_ref[at] = low
 
 
-def phase_tables(first_level, count, half, inner_bits, tile, tilt_ref):
+def phase_tables(first_level, count, half, inner_bits, tile, tilt_ref, cos_ref, sin_ref):
     bits = half.bit_length() - 1
     lane = iota((1, LANES), 1)
     angle = jnp.zeros((1, LANES), jnp.float32)
@@ -121,19 +114,70 @@
         tile_start = jnp.where(here, tile * 2**width, tile_start)
         for child in range(2):
             angle = jnp.where(
-                (lane >> 1) == 2 * level + child,
-                tilt_ref[2 * (first_level + level) + child],
-                angle,
+                (lane >> 1) == 2 * level + child, tilt_ref[child, first_level + level], angle
             )
     order = bit_reversed(iota((half, LANES), 0), bits)
     beam = tile_start + (order & mask)
     j_index = (2 * beam + (lane & 1)).astype(jnp.float32)
     phi = angle * ((j_index + 0.5) * step - 1.0)
     norm = 1.0 / math.sqrt(2.0)
-    return jnp.cos(phi) * norm, jnp.sin(phi) * norm
-
-
-def level_step(level, half, source, cos_t, sin_t, high_ref, low_ref):
+    cos_ref[...] = jnp.cos(phi) * norm
+    sin_ref[...] = jnp.sin(phi) * norm
+
+
+def compress_kernel(total_freq, local, echo_ref, matched_hbm, offsets_hbm, fraction_hbm, tilt_hbm,
+                    order_hbm, prof_ref, high_ref, low_ref, cos_ref, sin_ref, cos2_ref, sin2_ref,
+                    order_ref, table_ref, echo_buf, sum_ref, matched_ref, offsets_ref,
+                    fraction_ref, tilt_ref, sems, small_sems):
+    pulses, tiles = echo_ref.shape[:2]
+    freq = tiles * LANES
+    copies = [
+        pltpu.make_async_copy(echo_ref.at[:, n], echo_buf.at[n], sems.at[n]) for n in range(tiles)
+    ]
+    pairs = (
+        (matched_hbm, matched_ref),
+        (offsets_hbm, offsets_ref),
+        (fraction_hbm, fraction_ref),
+        (tilt_hbm, tilt_ref),
+        (order_hbm, order_ref),
+    )
+    small = [pltpu.make_async_copy(*pair, small_sems.at[n]) for n, pair in enumerate(pairs)]
+    for copy in small + copies:
+        copy.start()
+    bands, apertures = lax.axis_size("band"), lax.axis_size("aperture")
+    band = lax.axis_index("band")
+    levels = high_ref.shape[0] // 2
+    small[0].wait()
+    make_table(total_freq, band * freq, matched_ref, table_ref)
+    for copy in small[1:]:
+        copy.wait()
+    build_matrices(levels, offsets_ref, fraction_ref, high_ref, low_ref)
+    phase_tables(0, local, cos_ref.shape[0], 0, 0, tilt_ref, cos_ref, sin_ref)
+    devices = bands * apertures
+    tile = bit_reversed(lax.axis_index("aperture") * bands + band, devices.bit_length() - 1)
+    inner = (pulses // devices).bit_length() - 1
+    rest = levels - local
+    phase_tables(local, rest, cos2_ref.shape[0], inner, tile, tilt_ref, cos2_ref, sin2_ref)
+    for copy in copies:
+        copy.wait()
+    echoes = jnp.concatenate(
+        [echo_buf.at[n].reshape(2 * pulses, LANES)[...] for n in range(tiles)], axis=1
+    )
+    dims = (((1,), (1,)), ((), ()))
+    sums = lax.dot_general(echoes, table_ref[...], dims, preferred_element_type=jnp.float32)
+    sum_ref[0] = sums[:, 0:R]
+    sum_ref[1] = sums[:, R:]
+    even, odd = pl.ds(0, pulses, stride=2), pl.ds(1, pulses, stride=2)
+    re = sum_ref[0, even, :] - sum_ref[1, odd, :]
+    im = sum_ref[1, even, :] + sum_ref[0, odd, :]
+    for part, value in enumerate((re, im)):
+        high, low = halves_of(value)
+        prof_ref[0:pulses, part * R : (part + 1) * R] = high
+        prof_ref[pulses:, part * R : (part + 1) * R] = low
+
+
+def level_step(level, half, source, tables, high_ref, low_ref):
+    cos_ref, sin_ref = tables
     products = []
     for child in range(2):
         held = source[pl.ds(child, 2 * half, stride=2), :]
@@ -146,8 +190,8 @@
         re = im = None
         for child in range(2):
             entry = 4 * level + 2 * child + parity
-            co = cos_t[:, entry : entry + 1]
-            si = sin_t[:, entry : entry + 1]
+            co = cos_ref[:, entry : entry + 1]
+            si = sin_ref[:, entry : entry + 1]
             p_re = products[child][0:half, parity * R : (parity + 1) * R]
             p_im = products[child][half:, parity * R : (parity + 1) * R]
             r_new = p_re * co - p_im * si
@@ -161,25 +205,29 @@
 def local_kernel(count, devices, *refs):
     bands = lax.axis_size("band")
     orders = refs[:bands]
-    prof_ref, offsets_ref, fraction_ref, tilt_ref = refs[bands : bands + 4]
-    out_ref, high_ref, low_ref, image_ref = refs[bands + 4 :]
+    prof_ref, high_ref, low_ref, cos_ref, sin_ref, out_ref, image_ref = refs[bands:]
     pulses = prof_ref.shape[0] // 2
     half = pulses // 2
     group = pulses // bands
-    build_matrices(0, count, offsets_ref, fraction_ref, high_ref, low_ref)
-    cos_t, sin_t = phase_tables(0, count, half, 0, 0, tilt_ref)
     me = lax.axis_index("band")
     for apart in range(bands):
         start = pl.multiple_of((me ^ apart) * group, group)
-        for pulse in range(group):
-            row = start + orders[apart][pulse]
-            for part in range(0, 2 * pulses, pulses):
-                value = prof_ref[pl.ds(part + row, 1), :]
-                image_ref[0, pl.ds(part + start + pulse, 1), :] = value
+        order = orders[apart][...]
+        chosen = iota((group, group), 0) == jnp.broadcast_to(order, (group, group))
+        chosen = jnp.where(chosen, 1.0, 0.0).astype(jnp.bfloat16)
+        twice = jnp.concatenate([chosen, chosen], axis=0)
+        held = jnp.concatenate(
+            [prof_ref[pl.ds(start, group), :], prof_ref[pl.ds(pulses + start, group), :]], axis=0
+        )
+        moved = lax.dot_general(
+            twice, held, (((0,), (0,)), ((), ())), preferred_element_type=jnp.float32
+        )
+        image_ref[0, pl.ds(start, group), :] = moved[:, 0:R]
+        image_ref[0, pl.ds(pulses + start, group), :] = moved[:, R:]
     kept = pulses // devices
     for level in range(count):
         source, target = image_ref.at[level % 2], image_ref.at[(level + 1) % 2]
-        result = level_step(level, half, source, cos_t, sin_t, high_ref, low_ref)
+        result = level_step(level, half, source, (cos_ref, sin_ref), high_ref, low_ref)
         for parity in range(2):
             for part in range(2):
                 value = result[parity][part]
@@ -213,19 +261,14 @@
     return jnp.minimum(position, 2) + jnp.minimum(size - 1 - position, 2) + 1
 
 
-def final_kernel(first_level, count, recv_ref, offsets_ref, fraction_ref, tilt_ref, out_ref,
-                 high_ref, low_ref, image_ref, pad_ref):
+def final_kernel(first_level, count, recv_ref, high_ref, low_ref, cos_ref, sin_ref, out_ref,
+                 image_ref, pad_ref):
     bands, apertures = lax.axis_size("band"), lax.axis_size("aperture")
-    devices = bands * apertures
     rows = out_ref.shape[0]
     half = rows // 2
     kept = rows // apertures
-    tile_bits = devices.bit_length() - 1
-    inner = kept.bit_length() - 1
-    build_matrices(first_level, count, offsets_ref, fraction_ref, high_ref, low_ref)
-    place = lax.axis_index("aperture") * bands + lax.axis_index("band")
-    tile = bit_reversed(place, tile_bits)
-    cos_t, sin_t = phase_tables(first_level, count, half, inner, tile, tilt_ref)
+    high_ref = high_ref.at[2 * first_level : 2 * (first_level + count)]
+    low_ref = low_ref.at[2 * first_level : 2 * (first_level + count)]
     for part in range(2):
         for beam in range(kept):
             total = None
@@ -236,7 +279,7 @@
             image_ref[0, pl.ds(part * rows + beam * apertures, apertures), :] = total
     for level in range(count):
         source, target = image_ref.at[level % 2], image_ref.at[(level + 1) % 2]
-        result = level_step(level, half, source, cos_t, sin_t, high_ref, low_ref)
+        result = level_step(level, half, source, (cos_ref, sin_ref), high_ref, low_ref)
         for parity in range(2):
             for part in range(2):
                 target[pl.ds(part * rows + parity * half, half), :] = result[parity][part]
@@ -274,55 +317,79 @@
     group = pulse_order.shape[-1]
     levels = tilt_angle.shape[0]
     local = pulses.bit_length() - 1
-    order = pulse_order.reshape(group)
+    rest = levels - local
+    kept = pulses // devices
+    rows = kept * apertures
+    tiles = freq // LANES
+    order = pulse_order.reshape(1, group)
     orders = [order]
     for apart in range(1, bands):
         orders.append(lax.ppermute(order, "band", [(n, n ^ apart) for n in range(bands)]))
-    offsets, fraction = offsets.reshape(-1), fraction.reshape(-1)
-    tilt = tilt_angle.reshape(-1)
-    vmem, smem = pl.BlockSpec(memory_space=VMEM), pl.BlockSpec(memory_space=SMEM)
-    profiles = pl.pallas_call(
-        functools.partial(compress_kernel, matched.shape[1]),
-        out_shape=jax.ShapeDtypeStruct((2 * pulses, R), jnp.float32),
-        in_specs=[vmem, vmem],
-        out_specs=vmem,
-        scratch_shapes=[VMEM((2 * R, freq), jnp.bfloat16)],
+    vmem = pl.BlockSpec(memory_space=VMEM)
+    params = pltpu.CompilerParams(vmem_limit_bytes=16 * 2**20)
+    f32, bf16 = jnp.float32, jnp.bfloat16
+    shape_of = jax.ShapeDtypeStruct
+    views = (
+        raw_echoes.reshape(pulses, 2, tiles, LANES).transpose(0, 2, 1, 3),
+        matched,
+        offsets.transpose(1, 2, 3, 0),
+        fraction.transpose(1, 2, 0),
+        tilt_angle.transpose(1, 0),
+        order,
+    )
+    views = [pltpu.with_memory_space_constraint(view, pltpu.HBM) for view in views]
+    prof, high, low, cos_1, sin_1, cos_2, sin_2, orders[0] = pl.pallas_call(
+        functools.partial(compress_kernel, matched.shape[1], local),
+        out_shape=[
+            shape_of((2 * pulses, 2 * R), bf16),
+            shape_of((2 * levels, R, 2 * R), bf16),
+            shape_of((2 * levels, R, 2 * R), bf16),
+            shape_of((pulses // 2, LANES), f32),
+            shape_of((pulses // 2, LANES), f32),
+            shape_of((rows // 2, LANES), f32),
+            shape_of((rows // 2, LANES), f32),
+            shape_of(order.shape, order.dtype),
+        ],
+        in_specs=[pl.BlockSpec(memory_space=pltpu.HBM)] * 6,
+        out_specs=[vmem] * 8,
+        scratch_shapes=[
+            VMEM((2 * R, freq), bf16),
+            VMEM((tiles, pulses, 2, LANES), bf16),
+            VMEM((2, 2 * pulses, R), f32),
+            VMEM(matched.shape, f32),
+            SMEM(views[2].shape, jnp.int32),
+            SMEM(views[3].shape, f32),
+            SMEM(views[4].shape, f32),
+            pltpu.SemaphoreType.DMA((tiles,)),
+            pltpu.SemaphoreType.DMA((5,)),
+        ],
         cost_estimate=pl.CostEstimate(
             flops=8 * pulses * freq * R, bytes_accessed=4 * pulses * freq, transcendentals=0
         ),
+        compiler_params=params,
         name="compress",
-    )(raw_echoes.reshape(pulses, 2 * freq), matched)
-    kept = pulses // devices
+    )(*views)
     sent = pl.pallas_call(
         functools.partial(local_kernel, local, devices),
-        out_shape=jax.ShapeDtypeStruct((devices * 2 * kept, R), jnp.float32),
-        in_specs=[smem] * bands + [vmem, smem, smem, smem],
+        out_shape=shape_of((devices * 2 * kept, R), f32),
+        in_specs=[vmem] * (bands + 5),
         out_specs=vmem,
-        scratch_shapes=[
-            VMEM((2 * local, R, 2 * R), jnp.bfloat16),
-            VMEM((2 * local, R, 2 * R), jnp.bfloat16),
-            VMEM((2, 2 * pulses, R), jnp.float32),
-        ],
+        scratch_shapes=[VMEM((2, 2 * pulses, R), f32)],
+        compiler_params=params,
         name="levels",
-    )(*orders, profiles, offsets, fraction, tilt)
+    )(*orders, prof, high, low, cos_1, sin_1)
     received = lax.all_to_all(
         sent.reshape(devices, 2 * kept, R), ("aperture", "band"), 0, 0, tiled=True
     ).reshape(devices * 2 * kept, R)
-    rows = kept * apertures
-    rest = levels - local
     return pl.pallas_call(
         functools.partial(final_kernel, local, rest),
-        out_shape=jax.ShapeDtypeStruct((rows, R), jnp.float32),
-        in_specs=[vmem, smem, smem, smem],
+        out_shape=shape_of((rows, R), f32),
+        in_specs=[vmem] * 5,
         out_specs=vmem,
-        scratch_shapes=[
-            VMEM((2 * rest, R, 2 * R), jnp.bfloat16),
-            VMEM((2 * rest, R, 2 * R), jnp.bfloat16),
-            VMEM((2, 2 * rows, R), jnp.float32),
-            VMEM((2, rows + 16, R), jnp.float32),
-        ],
+        scratch_shapes=[VMEM((2, 2 * rows, R), f32), VMEM((2, rows + 16, R), f32)],
+        compiler_params=params,
         name="finish",
-    )(received, offsets, fraction, tilt)
+    )(received, high, low, cos_2, sin_2)
 
 
 def solution(mesh):

time: 33.2 us -> 25.6 us (0.77)
  local copies, waits for them, and re-layouts: 6.04 us -> 0 us
  Pallas kernels: 9.32 us -> 8.2 us
    unnamed x18 -> x0, local copies, waits for them, and re-layouts: 4.05 us -> none
    pallas_call x1, Pallas kernels: 4.26 us -> 1.94 us  [body(): pl.pallas_call(functools.partial(local_kernel, local, devices), out_shape...]
    reshape x3 -> x0, local copies, waits for them, and re-layouts: 1.99 us -> none  [the longest x2 1.31 us: body(): offsets, fraction = (offsets.reshape(-1), fraction.reshape(-1))]
    pallas_call x2, Pallas kernels: 5.06 us -> 6.27 us  [the longest x1 4.91 us: body(): pl.pallas_call(functools.partial(compress_kernel, matched.shape[1], local...]
  transfers between devices with their start and end apart: 3 -> 3, of which waited for: 0 -> 0; matrix products, arithmetic and copies ran while one was open for 13% -> 0% of each run, Pallas kernels for 7% -> 19%
where the time goes in v2:
time: 25.6 us; the launch traced here: 25.4 us
  blocking collectives  14.1 us (55%)
  Pallas kernels  8.2 us (32%)
  starting transfers between devices  3.11 us (12%)
    all_to_all x1, blocking collectives, body(): lax.all_to_all(sent.reshape(devices, 2 * kept, R), ('aperture', 'band'),...  14.1 us
    pallas_call x1, Pallas kernels, body(): pl.pallas_call(functools.partial(compress_kernel, matched.shape[1], local...  4.91 us
    ppermute x3, starting transfers between devices, body(): lax.ppermute(order, 'band', [(n, n ^ apart) for n in range(bands)])  3.11 us
    pallas_call x1, Pallas kernels, body(): pl.pallas_call(functools.partial(local_kernel, local, devices), out_shape...  1.94 us
    pallas_call x1, Pallas kernels, body(): pl.pallas_call(functools.partial(final_kernel, local, rest), out_shape=sh...  1.36 us
  transfers between devices with their start and end apart: 3, of which 0 were waited for; matrix products, arithmetic and copies ran while one was open for 0% of the time, Pallas kernels for 19%

profile of v2, /device:TPU:0, one launch (start us, length us, event | category | flops | bytes accessed | tf_op | source)
XLA Modules:
  0.0 25.4 jit_solution(16647559315650763220)
XLA Ops:
  0.0 2.4 %collective-permute-start.2 = (s32[1,32]{1,0:T(1,128)}, s32[1,32]{1,0:T(1,128)S(1)}, u32[]{:S(2)}, u32[]{:S(2)}) collective-permute-start(s32[1,32]{1,0:T(1,128)} %bitcast.15), channel_id=1, source_target_pairs={{0,24},{8,16},{16,8},{24,0},{1,25},{9,17},{17,9},{25,1},{2,26},{10... | collective-permute-start | bytes 392 | tf_op jit(solution)/shard_map/ppermute | solution.py:327
  2.4 0.6 %collective-permute-start.1 = (s32[1,32]{1,0:T(1,128)}, s32[1,32]{1,0:T(1,128)S(1)}, u32[]{:S(2)}, u32[]{:S(2)}) collective-permute-start(s32[1,32]{1,0:T(1,128)} %bitcast.16), channel_id=1, source_target_pairs={{0,16},{8,24},{16,0},{24,8},{1,17},{9,25},{17,1},{25,9},{2,18},{10... | collective-permute-start | bytes 392 | tf_op jit(solution)/shard_map/ppermute | solution.py:327
  3.0 0.1 collective-permute-start
  3.1 4.9 %compress.1 = (bf16[256,256]{1,0:T(8,128)(2,1)S(1)}, bf16[20,128,256]{2,1,0:T(8,128)(2,1)S(1)}, bf16[20,128,256]{2,1,0:T(8,128)(2,1)S(1)}, f32[64,128]{1,0:T(8,1...) custom-call(bf16[128,8,2,128]{3,2,1,0:T(2,128)(2,1)} %bitcast.11, ...), custom_call_target="tpu_custom_call" | custom-call | flops 134217728 | bytes 524288 | tf_op jit(solution)/shard_map/compress/pallas_call | solution.py:341
  8.0 0.0 collective-permute-done.2.refs_3_
  8.0 0.0 collective-permute-done.1.refs_2_
  8.1 0.0 collective-permute-done.refs_1_
  8.1 1.9 %levels.1 = f32[256,128]{1,0:T(8,128)S(1)} custom-call(s32[1,32]{1,0:T(1,128)S(1)} %get-tuple-element.13.refs_0_, s32[1,32]{1,0:T(1,128)S(1)} %collective-permute-done.refs_1_, s32[1,32]{1,0:T(1,128)S(1)} %collective-permute-done.1.refs_2_, s32[1,32]{1,0:T(1,128)S(1)} %collective-permute-done.2.refs_3_, bf16[256,256]{1,0:T(8,128)(2,1)S(1)} %get-tuple-element.14.refs_4_, ...), custom_call_target="tpu_custom_call" | custom-call | tf_op jit(solution)/shard_map/levels/pallas_call | solution.py:372
  10.0 14.1 %all_to_all.5 = f32[32,8,128]{2,1,0:T(8,128)S(1)} all-to-all(f32[32,8,128]{2,1,0:T(8,128)S(1)} %bitcast.9), channel_id=1, replica_groups=mesh['band'=4,'aperture'=8] {'aperture','band'}, dimensions={0} | all-to-all | bytes 262144 | tf_op jit(solution)/shard_map/all_to_all | solution.py:381
  24.1 1.4 %finish.1 = f32[32,128]{1,0:T(8,128)} custom-call(f32[256,128]{1,0:T(8,128)S(1)} %bitcast.10, bf16[20,128,256]{2,1,0:T(8,128)(2,1)S(1)} %get-tuple-element.15.refs_5_.high_ref, bf16[20,128,256]{2,1,0:T(8,128)(2,1)S(1)} %get-tuple-element.16.refs_6_.low_ref, f32[16,128]{1,0:T(8,128)S(1)} %get-tuple-element.19.cos_ref, f32[16,128]{1,0:T(8,128)S(1)} %get-tuple-element.20.sin_ref), custom_call_target="tpu_custom_call" | custom-call | tf_op jit(solution)/shard_map/finish/pallas_call | solution.py:384
Async XLA Ops:
  0.0 8.0 %collective-permute-start.2 = (s32[1,32]{1,0:T(1,128)}, s32[1,32]{1,0:T(1,128)S(1)}, u32[]{:S(2)}, u32[]{:S(2)}) collective-permute-start(s32[1,32]{1,0:T(1,128)} %bitcast.15), channel_id=1, source_target_pairs={{0,24},{8,16},{16,8},{24,0},{1,25},{9,17},{17,9},{25,1},{2,26},{10... | collective-permute-start | bytes 392 | tf_op jit(solution)/shard_map/ppermute | solution.py:327
  2.4 5.6 %collective-permute-start.1 = (s32[1,32]{1,0:T(1,128)}, s32[1,32]{1,0:T(1,128)S(1)}, u32[]{:S(2)}, u32[]{:S(2)}) collective-permute-start(s32[1,32]{1,0:T(1,128)} %bitcast.16), channel_id=1, source_target_pairs={{0,16},{8,24},{16,0},{24,8},{1,17},{9,25},{17,1},{25,9},{2,18},{10... | collective-permute-start | bytes 392 | tf_op jit(solution)/shard_map/ppermute | solution.py:327
  3.0 5.1 %collective-permute-start = (s32[1,32]{1,0:T(1,128)}, s32[1,32]{1,0:T(1,128)S(1)}, u32[]{:S(2)}, u32[]{:S(2)}) collective-permute-start(s32[1,32]{1,0:T(1,128)} %bitcast.17), channel_id=1, source_target_pairs={{0,8},{8,0},{16,24},{24,16},{1,9},{9,1},{17,25},{25,17},{2,10},{10... | collective-permute-start | bytes 392 | tf_op jit(solution)/shard_map/ppermute | solution.py:327

commit v3 on v2

--- a/solution.py
+++ b/solution.py
@@ -32,43 +32,49 @@
     return high, low
 
 
+def cmul(first, second):
+    return (
+        first[0] * second[0] - first[1] * second[1],
+        first[0] * second[1] + first[1] * second[0],
+    )
+
+
 def make_table(total_freq, start, matched_ref, table_ref):
-    freq = table_ref.shape[1]
+    chunks = table_ref.shape[0]
     scale = 1.0 / math.sqrt(total_freq)
     turn = 2.0 * math.pi / total_freq
-    for chunk in range(freq // LANES):
-        first = start + chunk * LANES
-        lanes = pl.ds(pl.multiple_of(first, LANES), LANES)
-        f_index = first + iota((8, LANES), 1)
-        angle = ((f_index * iota((8, LANES), 0)) % total_freq).astype(jnp.float32) * turn
-        cos_a, sin_a = jnp.cos(angle), jnp.sin(angle)
-        angle = ((f_index * 8) % total_freq).astype(jnp.float32) * turn
-        cos_w, sin_w = jnp.cos(angle), jnp.sin(angle)
-        spec_r = matched_ref[0:1, lanes] * scale
-        spec_i = matched_ref[1:2, lanes] * scale
-        low_r = spec_r * cos_a - spec_i * sin_a
-        low_i = spec_r * sin_a + spec_i * cos_a
-        re = jnp.concatenate([low_r, low_r * cos_w - low_i * sin_w], axis=0)
-        im = jnp.concatenate([low_i, low_r * sin_w + low_i * cos_w], axis=0)
-        two_r = cos_w * cos_w - sin_w * sin_w
-        two_i = 2.0 * cos_w * sin_w
-        two_r = jnp.concatenate([two_r, two_r], axis=0)
-        two_i = jnp.concatenate([two_i, two_i], axis=0)
-        here = pl.ds(chunk * LANES, LANES)
-        for block in range(R // 16):
-            table_ref[pl.ds(block * 16, 16), here] = re.astype(jnp.bfloat16)
-            table_ref[pl.ds(R + block * 16, 16), here] = im.astype(jnp.bfloat16)
-            if block + 1 < R // 16:
-                re, im = re * two_r - im * two_i, re * two_i + im * two_r
-
-
-def build_matrices(levels, offsets_ref, fraction_ref, high_ref, low_ref):
-    lane = iota((8, LANES), 1)
-    tap = jnp.where(lane < LANES // 2, -lane, LANES - lane).astype(jnp.float32)
-    row = iota((8, LANES), 0)
+    rows = -(-chunks // 8) * 8
+    f_index = start + iota((rows, LANES), 0) * LANES + iota((rows, LANES), 1)
+    angle = f_index.astype(jnp.float32) * turn
+    cos_1, sin_1 = jnp.cos(angle), jnp.sin(angle)
+    sub = iota((8, LANES), 0)
+    for chunk in range(chunks):
+        lanes = pl.ds(pl.multiple_of(start + chunk * LANES, LANES), LANES)
+        power = [
+            jnp.broadcast_to(part[chunk : chunk + 1, :], (8, LANES)) for part in (cos_1, sin_1)
+        ]
+        spec = matched_ref[:, lanes] * scale
+        low = tuple(jnp.broadcast_to(spec[n : n + 1, :], (8, LANES)) for n in range(2))
+        for bit in range(3):
+            chosen = (sub >> bit) & 1 == 1
+            low = cmul(low, (jnp.where(chosen, power[0], 1.0), jnp.where(chosen, power[1], 0.0)))
+            power = cmul(power, power)
+        block = [jnp.concatenate(parts, axis=0) for parts in zip(low, cmul(low, power))]
+        power = cmul(power, power)
+        power = [jnp.concatenate([part, part], axis=0) for part in power]
+        for begin in range(0, R, 16):
+            table_ref[chunk, begin : begin + 16, :] = block[0].astype(jnp.bfloat16)
+            table_ref[chunk, R + begin : R + begin + 16, :] = block[1].astype(jnp.bfloat16)
+            if begin + 16 < R:
+                block = cmul(block, power)
+
+
+def build_matrices(levels, offsets_ref, fraction_ref, start_ref, band_ref, high_ref, low_ref):
+    period = 4 * SHIFT
+    lane, row = iota((8, LANES), 1), iota((8, LANES), 0)
+    near_tap = lane & (period - 1)
+    tap = jnp.where(near_tap < period // 2, -near_tap, period - near_tap).astype(jnp.float32)
     entries = [(n, c, p) for n in range(levels) for c in range(2) for p in range(2)]
-    edge = 2 * SHIFT
-    out_bin, in_bin = iota((edge, R), 1), iota((edge, R), 0)
     for block in range(0, len(entries), 8):
         here = entries[block : block + 8]
         shift = jnp.zeros((8, LANES), jnp.float32)
@@ -83,23 +89,33 @@
         for sub, (level, child, parity) in enumerate(here):
             moved = offsets_ref[child, parity, 0, level] - SHIFT
             one = jnp.broadcast_to(taper[sub : sub + 1, :], (8, LANES))
-            one = pltpu.roll(one, (LANES - moved) % LANES, 1)
-            wide = jnp.broadcast_to(one[0:1, :], (R, LANES))
-            wide = pltpu.roll(wide, 0, 1, stride=1, stride_axis=0)
-            window = in_bin - moved
-            keep = (window >= 0) & (jnp.abs(window - out_bin) <= 4)
-            top = jnp.where(keep, wide[0:edge], 0.0)
-            window = window + (R - edge)
-            keep = (window < R) & (jnp.abs(window - out_bin) <= 4)
-            bottom = jnp.where(keep, wide[R - edge :], 0.0)
-            wide = jnp.concatenate([top, wide[edge : R - edge], bottom], axis=0)
-            high, low = halves_of(wide)
-            at = (2 * level + child, slice(None), pl.ds(parity * LANES, LANES))
-            high_ref[at] = high
-            low_ref[at] = low
-
-
-def phase_tables(first_level, count, half, inner_bits, tile, tilt_ref, cos_ref, sin_ref):
+            one = pltpu.roll(one, (LANES - moved) & (LANES - 1), 1)
+            start_ref[block + sub] = pltpu.roll(one, 0, 1, stride=1, stride_axis=0)
+    for begin in range(0, R, 8):
+        first = begin - SHIFT - 4
+        inside = (lane >= first) & (lane < first + period)
+        band_ref[begin // 8] = jnp.where(inside, 1.0, 0.0)
+    for entry, (level, child, parity) in enumerate(entries):
+        moved = offsets_ref[child, parity, 0, level] - SHIFT
+        one = start_ref[entry]
+        turned = [one] + [pltpu.roll(one, begin, 1) for begin in range(8, period, 8)]
+        halves = []
+        for value in turned:
+            high = value.astype(jnp.bfloat16).astype(jnp.float32)
+            halves.append((high, value - high))
+        first = jnp.where(row >= moved, band_ref[0], 0.0)
+        last = jnp.where(row < moved + 8, band_ref[R // 8 - 1], 0.0)
+        for begin in range(0, R, 16):
+            for part, ref in enumerate((high_ref, low_ref)):
+                tiles = []
+                for tile in (begin // 8, begin // 8 + 1):
+                    keep = first if tile == 0 else last if tile == R // 8 - 1 else band_ref[tile]
+                    tiles.append(halves[tile % len(halves)][part] * keep)
+                ref[entry, begin : begin + 16, :] = jnp.concatenate(tiles, 0).astype(jnp.bfloat16)
+
+
+def phase_tables(first_level, count, inner_bits, tile, tilt_ref, cos_ref, sin_ref):
+    half = cos_ref.shape[0]
     bits = half.bit_length() - 1
     lane = iota((1, LANES), 1)
     angle = jnp.zeros((1, LANES), jnp.float32)
@@ -116,19 +132,26 @@
             angle = jnp.where(
                 (lane >> 1) == 2 * level + child, tilt_ref[child, first_level + level], angle
             )
-    order = bit_reversed(iota((half, LANES), 0), bits)
-    beam = tile_start + (order & mask)
+    norm = 1.0 / math.sqrt(2.0)
+    beam = tile_start + (bit_reversed(iota((8, LANES), 0), bits) & mask)
     j_index = (2 * beam + (lane & 1)).astype(jnp.float32)
     phi = angle * ((j_index + 0.5) * step - 1.0)
-    norm = 1.0 / math.sqrt(2.0)
-    cos_ref[...] = jnp.cos(phi) * norm
-    sin_ref[...] = jnp.sin(phi) * norm
+    inner = (jnp.cos(phi) * norm, jnp.sin(phi) * norm)
+    groups = half // 8
+    shape = (-(-groups // 8) * 8, LANES)
+    beam = bit_reversed(iota(shape, 0) << 3, bits) & mask
+    phi = angle * ((2 * beam).astype(jnp.float32) * step)
+    outer = (jnp.cos(phi), jnp.sin(phi))
+    for group in range(groups):
+        co, si = cmul(inner, [part[group : group + 1, :] for part in outer])
+        cos_ref[8 * group : 8 * group + 8, :] = co
+        sin_ref[8 * group : 8 * group + 8, :] = si
 
 
 def compress_kernel(total_freq, local, echo_ref, matched_hbm, offsets_hbm, fraction_hbm, tilt_hbm,
                     order_hbm, prof_ref, high_ref, low_ref, cos_ref, sin_ref, cos2_ref, sin2_ref,
-                    order_ref, table_ref, echo_buf, sum_ref, matched_ref, offsets_ref,
-                    fraction_ref, tilt_ref, sems, small_sems):
+                    order_ref, table_ref, echo_buf, line_buf, sum_ref, start_ref, band_ref, matched_ref, offsets_ref,
+                    fraction_ref, tilt_ref, sems, line_sems, small_sems):
     pulses, tiles = echo_ref.shape[:2]
     freq = tiles * LANES
     copies = [
@@ -146,25 +169,32 @@
         copy.start()
     bands, apertures = lax.axis_size("band"), lax.axis_size("aperture")
     band = lax.axis_index("band")
-    levels = high_ref.shape[0] // 2
+    levels = high_ref.shape[0] // 4
     small[0].wait()
     make_table(total_freq, band * freq, matched_ref, table_ref)
-    for copy in small[1:]:
+    for copy in small[1:] + copies:
         copy.wait()
-    build_matrices(levels, offsets_ref, fraction_ref, high_ref, low_ref)
-    phase_tables(0, local, cos_ref.shape[0], 0, 0, tilt_ref, cos_ref, sin_ref)
+    copies = [
+        pltpu.make_async_copy(
+            echo_buf.at[n].reshape(2 * pulses, LANES), line_buf.at[n], line_sems.at[n]
+        )
+        for n in range(tiles)
+    ]
+    for copy in copies:
+        copy.start()
+    build_matrices(levels, offsets_ref, fraction_ref, start_ref, band_ref, high_ref, low_ref)
+    phase_tables(0, local, 0, 0, tilt_ref, cos_ref, sin_ref)
     devices = bands * apertures
     tile = bit_reversed(lax.axis_index("aperture") * bands + band, devices.bit_length() - 1)
     inner = (pulses // devices).bit_length() - 1
     rest = levels - local
-    phase_tables(local, rest, cos2_ref.shape[0], inner, tile, tilt_ref, cos2_ref, sin2_ref)
+    phase_tables(local, rest, inner, tile, tilt_ref, cos2_ref, sin2_ref)
     for copy in copies:
         copy.wait()
-    echoes = jnp.concatenate(
-        [echo_buf.at[n].reshape(2 * pulses, LANES)[...] for n in range(tiles)], axis=1
-    )
+    echoes = jnp.concatenate([line_buf[n] for n in range(tiles)], axis=1)
     dims = (((1,), (1,)), ((), ()))
-    sums = lax.dot_general(echoes, table_ref[...], dims, preferred_element_type=jnp.float32)
+    table = jnp.concatenate([table_ref[n] for n in range(tiles)], axis=1)
+    sums = lax.dot_general(echoes, table, dims, preferred_element_type=jnp.float32)
     sum_ref[0] = sums[:, 0:R]
     sum_ref[1] = sums[:, R:]
     even, odd = pl.ds(0, pulses, stride=2), pl.ds(1, pulses, stride=2)
@@ -172,8 +202,8 @@
     im = sum_ref[1, even, :] + sum_ref[0, odd, :]
     for part, value in enumerate((re, im)):
         high, low = halves_of(value)
-        prof_ref[0:pulses, part * R : (part + 1) * R] = high
-        prof_ref[pulses:, part * R : (part + 1) * R] = low
+        prof_ref[part, 0:pulses, :] = high
+        prof_ref[part, pulses:, :] = low
 
 
 def level_step(level, half, source, tables, high_ref, low_ref):
@@ -182,9 +212,14 @@
     for child in range(2):
         held = source[pl.ds(child, 2 * half, stride=2), :]
         high, low = halves_of(held)
-        m_high, m_low = high_ref[2 * level + child], low_ref[2 * level + child]
+        at = 4 * level + 2 * child
+        m_high, m_low = (
+            jnp.concatenate([ref[at], ref[at + 1]], axis=1) for ref in (high_ref, low_ref)
+        )
         dot = functools.partial(jnp.dot, preferred_element_type=jnp.float32)
-        products.append(dot(high, m_high) + (dot(low, m_high) + dot(high, m_low)))
+        both = jnp.concatenate([high, low], axis=1)
+        m_both = jnp.concatenate([m_high, m_high], axis=0)
+        products.append(dot(both, m_both) + dot(high, m_low))
     result = []
     for parity in range(2):
         re = im = None
@@ -206,7 +241,7 @@
     bands = lax.axis_size("band")
     orders = refs[:bands]
     prof_ref, high_ref, low_ref, cos_ref, sin_ref, out_ref, image_ref = refs[bands:]
-    pulses = prof_ref.shape[0] // 2
+    pulses = prof_ref.shape[1] // 2
     half = pulses // 2
     group = pulses // bands
     me = lax.axis_index("band")
@@ -217,7 +252,13 @@
         chosen = jnp.where(chosen, 1.0, 0.0).astype(jnp.bfloat16)
         twice = jnp.concatenate([chosen, chosen], axis=0)
         held = jnp.concatenate(
-            [prof_ref[pl.ds(start, group), :], prof_ref[pl.ds(pulses + start, group), :]], axis=0
+            [
+                jnp.concatenate(
+                    [prof_ref[part, pl.ds(side + start, group), :] for side in (0, pulses)], axis=0
+                )
+                for part in range(2)
+            ],
+            axis=1,
         )
         moved = lax.dot_general(
             twice, held, (((0,), (0,)), ((), ())), preferred_element_type=jnp.float32
@@ -267,8 +308,8 @@
     rows = out_ref.shape[0]
     half = rows // 2
     kept = rows // apertures
-    high_ref = high_ref.at[2 * first_level : 2 * (first_level + count)]
-    low_ref = low_ref.at[2 * first_level : 2 * (first_level + count)]
+    high_ref = high_ref.at[4 * first_level : 4 * (first_level + count)]
+    low_ref = low_ref.at[4 * first_level : 4 * (first_level + count)]
     for part in range(2):
         for beam in range(kept):
             total = None
@@ -341,9 +382,9 @@
     prof, high, low, cos_1, sin_1, cos_2, sin_2, orders[0] = pl.pallas_call(
         functools.partial(compress_kernel, matched.shape[1], local),
         out_shape=[
-            shape_of((2 * pulses, 2 * R), bf16),
-            shape_of((2 * levels, R, 2 * R), bf16),
-            shape_of((2 * levels, R, 2 * R), bf16),
+            shape_of((2, 2 * pulses, R), bf16),
+            shape_of((4 * levels, R, R), bf16),
+            shape_of((4 * levels, R, R), bf16),
             shape_of((pulses // 2, LANES), f32),
             shape_of((pulses // 2, LANES), f32),
             shape_of((rows // 2, LANES), f32),
@@ -353,13 +394,17 @@
         in_specs=[pl.BlockSpec(memory_space=pltpu.HBM)] * 6,
         out_specs=[vmem] * 8,
         scratch_shapes=[
-            VMEM((2 * R, freq), bf16),
+            VMEM((tiles, 2 * R, LANES), bf16),
             VMEM((tiles, pulses, 2, LANES), bf16),
+            VMEM((tiles, 2 * pulses, LANES), bf16),
             VMEM((2, 2 * pulses, R), f32),
+            VMEM((4 * levels, 8, LANES), f32),
+            VMEM((R // 8, 8, LANES), f32),
             VMEM(matched.shape, f32),
             SMEM(views[2].shape, jnp.int32),
             SMEM(views[3].shape, f32),
             SMEM(views[4].shape, f32),
+            pltpu.SemaphoreType.DMA((tiles,)),
             pltpu.SemaphoreType.DMA((tiles,)),
             pltpu.SemaphoreType.DMA((5,)),
         ],

time: 25.6 us -> 23.5 us (0.918)
  Pallas kernels: 8.2 us -> 6.09 us
    pallas_call x1, Pallas kernels: 4.91 us -> 3.07 us  [body(): pl.pallas_call(functools.partial(compress_kernel, matched.shape[1], local...]
  transfers between devices with their start and end apart: 3 -> 3, of which waited for: 0 -> 0; matrix products, arithmetic and copies ran while one was open for 0% -> 0% of each run, Pallas kernels for 19% -> 13%
where the time goes in v3:
time: 23.5 us; the launch traced here: 23.3 us
  blocking collectives  14.1 us (60%)
  Pallas kernels  6.09 us (26%)
  starting transfers between devices  3.11 us (13%)
    all_to_all x1, blocking collectives, body(): lax.all_to_all(sent.reshape(devices, 2 * kept, R), ('aperture', 'band'),...  14.1 us
    ppermute x3, starting transfers between devices, body(): lax.ppermute(order, 'band', [(n, n ^ apart) for n in range(bands)])  3.11 us
    pallas_call x1, Pallas kernels, body(): pl.pallas_call(functools.partial(compress_kernel, matched.shape[1], local...  3.07 us
    pallas_call x1, Pallas kernels, body(): pl.pallas_call(functools.partial(local_kernel, local, devices), out_shape...  1.7 us
    pallas_call x1, Pallas kernels, body(): pl.pallas_call(functools.partial(final_kernel, local, rest), out_shape=sh...  1.33 us
  transfers between devices with their start and end apart: 3, of which 0 were waited for; matrix products, arithmetic and copies ran while one was open for 0% of the time, Pallas kernels for 13%

profile of v3, /device:TPU:0, one launch (start us, length us, event | category | flops | bytes accessed | tf_op | source)
XLA Modules:
  0.0 23.3 jit_solution(969937876249361088)
XLA Ops:
  0.0 2.4 %collective-permute-start.2 = (s32[1,32]{1,0:T(1,128)}, s32[1,32]{1,0:T(1,128)S(1)}, u32[]{:S(2)}, u32[]{:S(2)}) collective-permute-start(s32[1,32]{1,0:T(1,128)} %bitcast.15), channel_id=1, source_target_pairs={{0,24},{8,16},{16,8},{24,0},{1,25},{9,17},{17,9},{25,1},{2,26},{10... | collective-permute-start | bytes 392 | tf_op jit(solution)/shard_map/ppermute | solution.py:368
  2.4 0.6 %collective-permute-start.1 = (s32[1,32]{1,0:T(1,128)}, s32[1,32]{1,0:T(1,128)S(1)}, u32[]{:S(2)}, u32[]{:S(2)}) collective-permute-start(s32[1,32]{1,0:T(1,128)} %bitcast.16), channel_id=1, source_target_pairs={{0,16},{8,24},{16,0},{24,8},{1,17},{9,25},{17,1},{25,9},{2,18},{10... | collective-permute-start | bytes 392 | tf_op jit(solution)/shard_map/ppermute | solution.py:368
  3.0 0.1 collective-permute-start
  3.1 3.1 %compress.1 = (bf16[2,256,128]{2,1,0:T(8,128)(2,1)S(1)}, bf16[40,128,128]{2,1,0:T(8,128)(2,1)S(1)}, bf16[40,128,128]{2,1,0:T(8,128)(2,1)S(1)}, f32[64,128]{1,0:T...) custom-call(bf16[128,8,2,128]{3,2,1,0:T(2,128)(2,1)} %bitcast.11, ...), custom_call_target="tpu_custom_call" | custom-call | flops 134217728 | bytes 524288 | tf_op jit(solution)/shard_map/compress/pallas_call | solution.py:382
  6.2 0.0 collective-permute-done.2.refs_3_
  6.2 0.0 collective-permute-done.1.refs_2_
  6.2 0.0 collective-permute-done.refs_1_
  6.2 1.7 %levels.1 = f32[256,128]{1,0:T(8,128)S(1)} custom-call(s32[1,32]{1,0:T(1,128)S(1)} %get-tuple-element.13.refs_0_, s32[1,32]{1,0:T(1,128)S(1)} %collective-permute-done.refs_1_, s32[1,32]{1,0:T(1,128)S(1)} %collective-permute-done.1.refs_2_, s32[1,32]{1,0:T(1,128)S(1)} %collective-permute-done.2.refs_3_, bf16[2,256,128]{2,1,0:T(8,128)(2,1)S(1)} %get-tuple-element.14.refs_4_, ...), custom_call_target="tpu_custom_call" | custom-call | tf_op jit(solution)/shard_map/levels/pallas_call | solution.py:417
  7.9 14.1 %all_to_all.5 = f32[32,8,128]{2,1,0:T(8,128)S(1)} all-to-all(f32[32,8,128]{2,1,0:T(8,128)S(1)} %bitcast.9), channel_id=1, replica_groups=mesh['band'=4,'aperture'=8] {'aperture','band'}, dimensions={0} | all-to-all | bytes 262144 | tf_op jit(solution)/shard_map/all_to_all | solution.py:426
  22.0 1.3 %finish.1 = f32[32,128]{1,0:T(8,128)} custom-call(f32[256,128]{1,0:T(8,128)S(1)} %bitcast.10, bf16[40,128,128]{2,1,0:T(8,128)(2,1)S(1)} %get-tuple-element.15.refs_5_.high_ref, bf16[40,128,128]{2,1,0:T(8,128)(2,1)S(1)} %get-tuple-element.16.refs_6_.low_ref, f32[16,128]{1,0:T(8,128)S(1)} %get-tuple-element.19.cos_ref, f32[16,128]{1,0:T(8,128)S(1)} %get-tuple-element.20.sin_ref), custom_call_target="tpu_custom_call" | custom-call | tf_op jit(solution)/shard_map/finish/pallas_call | solution.py:429
Async XLA Ops:
  0.0 6.2 %collective-permute-start.2 = (s32[1,32]{1,0:T(1,128)}, s32[1,32]{1,0:T(1,128)S(1)}, u32[]{:S(2)}, u32[]{:S(2)}) collective-permute-start(s32[1,32]{1,0:T(1,128)} %bitcast.15), channel_id=1, source_target_pairs={{0,24},{8,16},{16,8},{24,0},{1,25},{9,17},{17,9},{25,1},{2,26},{10... | collective-permute-start | bytes 392 | tf_op jit(solution)/shard_map/ppermute | solution.py:368
  2.4 3.8 %collective-permute-start.1 = (s32[1,32]{1,0:T(1,128)}, s32[1,32]{1,0:T(1,128)S(1)}, u32[]{:S(2)}, u32[]{:S(2)}) collective-permute-start(s32[1,32]{1,0:T(1,128)} %bitcast.16), channel_id=1, source_target_pairs={{0,16},{8,24},{16,0},{24,8},{1,17},{9,25},{17,1},{25,9},{2,18},{10... | collective-permute-start | bytes 392 | tf_op jit(solution)/shard_map/ppermute | solution.py:368
  3.0 3.2 %collective-permute-start = (s32[1,32]{1,0:T(1,128)}, s32[1,32]{1,0:T(1,128)S(1)}, u32[]{:S(2)}, u32[]{:S(2)}) collective-permute-start(s32[1,32]{1,0:T(1,128)} %bitcast.17), channel_id=1, source_target_pairs={{0,8},{8,0},{16,24},{24,16},{1,9},{9,1},{17,25},{25,17},{2,10},{10... | collective-permute-start | bytes 392 | tf_op jit(solution)/shard_map/ppermute | solution.py:368

commit v4 on v3

--- a/solution.py
+++ b/solution.py
@@ -39,14 +39,18 @@
     )
 
 
-def make_table(total_freq, start, matched_ref, table_ref):
-    chunks = table_ref.shape[0]
-    scale = 1.0 / math.sqrt(total_freq)
+def unit_table(total_freq, start, chunks):
     turn = 2.0 * math.pi / total_freq
     rows = -(-chunks // 8) * 8
     f_index = start + iota((rows, LANES), 0) * LANES + iota((rows, LANES), 1)
     angle = f_index.astype(jnp.float32) * turn
-    cos_1, sin_1 = jnp.cos(angle), jnp.sin(angle)
+    return jnp.cos(angle), jnp.sin(angle)
+
+
+def make_table(total_freq, start, twiddles, matched_ref, table_ref):
+    chunks = table_ref.shape[0]
+    scale = 1.0 / math.sqrt(total_freq)
+    cos_1, sin_1 = twiddles
     sub = iota((8, LANES), 0)
     for chunk in range(chunks):
         lanes = pl.ds(pl.multiple_of(start + chunk * LANES, LANES), LANES)
@@ -69,11 +73,22 @@
                 block = cmul(block, power)
 
 
-def build_matrices(levels, offsets_ref, fraction_ref, start_ref, band_ref, high_ref, low_ref):
+def edge_bands():
+    lane = iota((8, LANES), 1)
+    period = 4 * SHIFT
+    result = []
+    for begin in range(0, R, 8):
+        first = begin - SHIFT - 4
+        result.append(jnp.where((lane >= first) & (lane < first + period), 1.0, 0.0))
+    return result
+
+
+def build_starts(levels, offsets_ref, fraction_ref, start_ref, edge_ref):
     period = 4 * SHIFT
     lane, row = iota((8, LANES), 1), iota((8, LANES), 0)
     near_tap = lane & (period - 1)
     tap = jnp.where(near_tap < period // 2, -near_tap, period - near_tap).astype(jnp.float32)
+    bands = edge_bands()
     entries = [(n, c, p) for n in range(levels) for c in range(2) for p in range(2)]
     for block in range(0, len(entries), 8):
         here = entries[block : block + 8]
@@ -91,34 +106,49 @@
             one = jnp.broadcast_to(taper[sub : sub + 1, :], (8, LANES))
             one = pltpu.roll(one, (LANES - moved) & (LANES - 1), 1)
             start_ref[block + sub] = pltpu.roll(one, 0, 1, stride=1, stride_axis=0)
-    for begin in range(0, R, 8):
-        first = begin - SHIFT - 4
-        inside = (lane >= first) & (lane < first + period)
-        band_ref[begin // 8] = jnp.where(inside, 1.0, 0.0)
-    for entry, (level, child, parity) in enumerate(entries):
-        moved = offsets_ref[child, parity, 0, level] - SHIFT
+            edge_ref[0, block + sub] = jnp.where(row >= moved, bands[0], 0.0)
+            edge_ref[1, block + sub] = jnp.where(row < moved + 8, bands[-1], 0.0)
+
+
+def build_angles(first_level, count, tilt_ref):
+    lane = iota((1, LANES), 1)
+    angle = jnp.zeros((1, LANES), jnp.float32)
+    for level in range(count):
+        for child in range(2):
+            angle = jnp.where(
+                (lane >> 1) == 2 * level + child, tilt_ref[child, first_level + level], angle
+            )
+    return angle
+
+
+def build_matrices(start_ref, edge_ref, band_ref, high_ref, low_ref):
+    period = 4 * SHIFT
+    for tile, band in enumerate(edge_bands()):
+        band_ref[tile] = band
+    last = R // 8 - 1
+    for entry in range(start_ref.shape[0]):
         one = start_ref[entry]
         turned = [one] + [pltpu.roll(one, begin, 1) for begin in range(8, period, 8)]
         halves = []
         for value in turned:
             high = value.astype(jnp.bfloat16).astype(jnp.float32)
             halves.append((high, value - high))
-        first = jnp.where(row >= moved, band_ref[0], 0.0)
-        last = jnp.where(row < moved + 8, band_ref[R // 8 - 1], 0.0)
         for begin in range(0, R, 16):
             for part, ref in enumerate((high_ref, low_ref)):
                 tiles = []
                 for tile in (begin // 8, begin // 8 + 1):
-                    keep = first if tile == 0 else last if tile == R // 8 - 1 else band_ref[tile]
+                    if tile in (0, last):
+                        keep = edge_ref[tile // last, entry]
+                    else:
+                        keep = band_ref[tile]
                     tiles.append(halves[tile % len(halves)][part] * keep)
                 ref[entry, begin : begin + 16, :] = jnp.concatenate(tiles, 0).astype(jnp.bfloat16)
 
 
-def phase_tables(first_level, count, inner_bits, tile, tilt_ref, cos_ref, sin_ref):
+def phase_tables(first_level, count, inner_bits, tile, angle, cos_ref, sin_ref):
     half = cos_ref.shape[0]
     bits = half.bit_length() - 1
     lane = iota((1, LANES), 1)
-    angle = jnp.zeros((1, LANES), jnp.float32)
     step = jnp.ones((1, LANES), jnp.float32)
     mask = jnp.zeros((1, LANES), jnp.int32)
     tile_start = jnp.zeros((1, LANES), jnp.int32)
@@ -128,10 +158,6 @@
         step = jnp.where(here, 2.0 ** -(first_level + level), step)
         mask = jnp.where(here, 2**width - 1, mask)
         tile_start = jnp.where(here, tile * 2**width, tile_start)
-        for child in range(2):
-            angle = jnp.where(
-                (lane >> 1) == 2 * level + child, tilt_ref[child, first_level + level], angle
-            )
     norm = 1.0 / math.sqrt(2.0)
     beam = tile_start + (bit_reversed(iota((8, LANES), 0), bits) & mask)
     j_index = (2 * beam + (lane & 1)).astype(jnp.float32)
@@ -148,10 +174,12 @@
         sin_ref[8 * group : 8 * group + 8, :] = si
 
 
-def compress_kernel(total_freq, local, echo_ref, matched_hbm, offsets_hbm, fraction_hbm, tilt_hbm,
-                    order_hbm, prof_ref, high_ref, low_ref, cos_ref, sin_ref, cos2_ref, sin2_ref,
-                    order_ref, table_ref, echo_buf, line_buf, sum_ref, start_ref, band_ref, matched_ref, offsets_ref,
-                    fraction_ref, tilt_ref, sems, line_sems, small_sems):
+def compress_kernel(total_freq, local, fold, *refs):
+    echo_ref, matched_hbm, offsets_hbm, fraction_hbm, tilt_hbm, order_hbm = refs[:6]
+    shares, refs = refs[6 : 6 + fold], refs[6 + fold :]
+    start_ref, edge_ref, angle_ref, order_ref = refs[:4]
+    table_ref, echo_buf, line_buf, sum_ref, matched_ref = refs[4:9]
+    offsets_ref, fraction_ref, tilt_ref, sems, line_sems, small_sems = refs[9:]
     pulses, tiles = echo_ref.shape[:2]
     freq = tiles * LANES
     copies = [
@@ -167,12 +195,16 @@
     small = [pltpu.make_async_copy(*pair, small_sems.at[n]) for n, pair in enumerate(pairs)]
     for copy in small + copies:
         copy.start()
-    bands, apertures = lax.axis_size("band"), lax.axis_size("aperture")
+    bands = lax.axis_size("band")
     band = lax.axis_index("band")
-    levels = high_ref.shape[0] // 4
-    small[0].wait()
-    make_table(total_freq, band * freq, matched_ref, table_ref)
-    for copy in small[1:] + copies:
+    levels = start_ref.shape[0] // 4
+    twiddles = unit_table(total_freq, band * freq, tiles)
+    for copy in small[1:]:
+        copy.wait()
+    build_starts(levels, offsets_ref, fraction_ref, start_ref, edge_ref)
+    angle_ref[0:1, :] = build_angles(0, local, tilt_ref)
+    angle_ref[1:2, :] = build_angles(local, levels - local, tilt_ref)
+    for copy in copies:
         copy.wait()
     copies = [
         pltpu.make_async_copy(
@@ -182,13 +214,8 @@
     ]
     for copy in copies:
         copy.start()
-    build_matrices(levels, offsets_ref, fraction_ref, start_ref, band_ref, high_ref, low_ref)
-    phase_tables(0, local, 0, 0, tilt_ref, cos_ref, sin_ref)
-    devices = bands * apertures
-    tile = bit_reversed(lax.axis_index("aperture") * bands + band, devices.bit_length() - 1)
-    inner = (pulses // devices).bit_length() - 1
-    rest = levels - local
-    phase_tables(local, rest, inner, tile, tilt_ref, cos2_ref, sin2_ref)
+    small[0].wait()
+    make_table(total_freq, band * freq, twiddles, matched_ref, table_ref)
     for copy in copies:
         copy.wait()
     echoes = jnp.concatenate([line_buf[n] for n in range(tiles)], axis=1)
@@ -197,13 +224,28 @@
     sums = lax.dot_general(echoes, table, dims, preferred_element_type=jnp.float32)
     sum_ref[0] = sums[:, 0:R]
     sum_ref[1] = sums[:, R:]
-    even, odd = pl.ds(0, pulses, stride=2), pl.ds(1, pulses, stride=2)
-    re = sum_ref[0, even, :] - sum_ref[1, odd, :]
-    im = sum_ref[1, even, :] + sum_ref[0, odd, :]
-    for part, value in enumerate((re, im)):
-        high, low = halves_of(value)
-        prof_ref[part, 0:pulses, :] = high
-        prof_ref[part, pulses:, :] = low
+    group = pulses // bands
+    held = bands // fold
+    for side in range(fold):
+        for member in range(held):
+            first = 2 * group * (member * fold + ((band ^ side) & (fold - 1)))
+            even = pl.ds(pl.multiple_of(first, 8), group, stride=2)
+            odd = pl.ds(first + 1, group, stride=2)
+            re = sum_ref[0, even, :] - sum_ref[1, odd, :]
+            im = sum_ref[1, even, :] + sum_ref[0, odd, :]
+            shares[side][0, member * group : (member + 1) * group, :] = re
+            shares[side][1, member * group : (member + 1) * group, :] = im
+
+
+def matrix_kernel(local, inner, start_ref, edge_ref, angle_ref, high_ref, low_ref,
+                  cos_ref, sin_ref, cos2_ref, sin2_ref, band_ref):
+    bands, apertures = lax.axis_size("band"), lax.axis_size("aperture")
+    levels = start_ref.shape[0] // 4
+    build_matrices(start_ref, edge_ref, band_ref, high_ref, low_ref)
+    phase_tables(0, local, 0, 0, angle_ref[0:1, :], cos_ref, sin_ref)
+    place = lax.axis_index("aperture") * bands + lax.axis_index("band")
+    tile = bit_reversed(place, (bands * apertures).bit_length() - 1)
+    phase_tables(local, levels - local, inner, tile, angle_ref[1:2, :], cos2_ref, sin2_ref)
 
 
 def level_step(level, half, source, tables, high_ref, low_ref):
@@ -237,51 +279,49 @@
     return result
 
 
-def local_kernel(count, devices, *refs):
-    bands = lax.axis_size("band")
-    orders = refs[:bands]
-    prof_ref, high_ref, low_ref, cos_ref, sin_ref, out_ref, image_ref = refs[bands:]
-    pulses = prof_ref.shape[1] // 2
-    half = pulses // 2
-    group = pulses // bands
-    me = lax.axis_index("band")
-    for apart in range(bands):
+def local_kernel(count, fold, *refs):
+    devices = lax.axis_size("band") * lax.axis_size("aperture")
+    held = lax.axis_size("band") // fold
+    orders, shares, refs = refs[:held], refs[held : held + fold], refs[held + fold :]
+    high_ref, low_ref, cos_ref, sin_ref, out_ref, image_ref = refs
+    rows = shares[0].shape[1]
+    half = rows // 2
+    group = rows // held
+    me = lax.axis_index("band") // fold
+    for apart in range(held):
         start = pl.multiple_of((me ^ apart) * group, group)
-        order = orders[apart][...]
-        chosen = iota((group, group), 0) == jnp.broadcast_to(order, (group, group))
+        chosen = iota((group, group), 0) == jnp.broadcast_to(orders[apart][...], (group, group))
         chosen = jnp.where(chosen, 1.0, 0.0).astype(jnp.bfloat16)
         twice = jnp.concatenate([chosen, chosen], axis=0)
-        held = jnp.concatenate(
-            [
-                jnp.concatenate(
-                    [prof_ref[part, pl.ds(side + start, group), :] for side in (0, pulses)], axis=0
-                )
-                for part in range(2)
-            ],
-            axis=1,
-        )
+        parts = []
+        for part in range(2):
+            value = shares[0][part, pl.ds(start, group), :]
+            for share in shares[1:]:
+                value = value + share[part, pl.ds(start, group), :]
+            parts.append(jnp.concatenate(halves_of(value), axis=0))
         moved = lax.dot_general(
-            twice, held, (((0,), (0,)), ((), ())), preferred_element_type=jnp.float32
+            twice,
+            jnp.concatenate(parts, axis=1),
+            (((0,), (0,)), ((), ())),
+            preferred_element_type=jnp.float32,
         )
         image_ref[0, pl.ds(start, group), :] = moved[:, 0:R]
-        image_ref[0, pl.ds(pulses + start, group), :] = moved[:, R:]
-    kept = pulses // devices
+        image_ref[0, pl.ds(rows + start, group), :] = moved[:, R:]
     for level in range(count):
         source, target = image_ref.at[level % 2], image_ref.at[(level + 1) % 2]
         result = level_step(level, half, source, (cos_ref, sin_ref), high_ref, low_ref)
         for parity in range(2):
             for part in range(2):
-                value = result[parity][part]
-                if level + 1 < count:
-                    target[pl.ds(part * pulses + parity * half, half), :] = value
-                    continue
-                size = min(half, devices)
-                for piece in range(half // size):
-                    row = parity * half + piece * size
-                    begin = (row % devices) * 2 * kept + part * kept + row // devices
-                    out_ref[pl.ds(begin, size, stride=2 * kept), :] = value[
-                        piece * size : (piece + 1) * size
-                    ]
+                target[pl.ds(part * rows + parity * half, half), :] = result[parity][part]
+    last = image_ref.at[count % 2]
+    per = rows // devices
+    for part in range(2):
+        for unit in range(per):
+            if fold == 1:
+                value = last[pl.ds(part * rows + unit * devices, devices), :]
+            else:
+                value = last[pl.ds(part * rows + unit, devices, stride=per), :]
+            out_ref[pl.ds(part * per + unit, devices, stride=2 * per), :] = value
 
 
 def box(rows):
@@ -302,22 +342,27 @@
     return jnp.minimum(position, 2) + jnp.minimum(size - 1 - position, 2) + 1
 
 
-def final_kernel(first_level, count, recv_ref, high_ref, low_ref, cos_ref, sin_ref, out_ref,
+def final_kernel(first_level, count, fold, recv_ref, high_ref, low_ref, cos_ref, sin_ref, out_ref,
                  image_ref, pad_ref):
     bands, apertures = lax.axis_size("band"), lax.axis_size("aperture")
     rows = out_ref.shape[0]
     half = rows // 2
-    kept = rows // apertures
+    per = recv_ref.shape[0] // (2 * bands * apertures)
     high_ref = high_ref.at[4 * first_level : 4 * (first_level + count)]
     low_ref = low_ref.at[4 * first_level : 4 * (first_level + count)]
     for part in range(2):
-        for beam in range(kept):
-            total = None
-            for band in range(bands):
-                begin = band * 2 * kept + part * kept + beam
-                value = recv_ref[pl.ds(begin, apertures, stride=bands * 2 * kept), :]
-                total = value if total is None else total + value
-            image_ref[0, pl.ds(part * rows + beam * apertures, apertures), :] = total
+        for unit in range(per):
+            for core in range(fold):
+                total = None
+                for band in range(core, bands, fold):
+                    begin = (band * 2 + part) * per + unit
+                    value = recv_ref[pl.ds(begin, apertures, stride=bands * 2 * per), :]
+                    total = value if total is None else total + value
+                if fold == 1:
+                    place = pl.ds(part * rows + unit * apertures, apertures)
+                else:
+                    place = pl.ds(part * rows + unit * fold + core, apertures, stride=bands)
+                image_ref[0, place, :] = total
     for level in range(count):
         source, target = image_ref.at[level % 2], image_ref.at[(level + 1) % 2]
         result = level_step(level, half, source, (cos_ref, sin_ref), high_ref, low_ref)
@@ -357,19 +402,22 @@
     pulses, _, freq = raw_echoes.shape
     group = pulse_order.shape[-1]
     levels = tilt_angle.shape[0]
-    local = pulses.bit_length() - 1
+    tiles = freq // LANES
+    fold = 2 if group == devices and bands % 2 == 0 else 1
+    held = bands // fold
+    rows = group * held
+    local = (rows if fold == 1 else group).bit_length() - 1
     rest = levels - local
-    kept = pulses // devices
-    rows = kept * apertures
-    tiles = freq // LANES
+    inner = local - (devices.bit_length() - 1)
+    per = rows // devices
+    f32, bf16 = jnp.float32, jnp.bfloat16
+    shape_of = jax.ShapeDtypeStruct
+    vmem = pl.BlockSpec(memory_space=VMEM)
+    params = pltpu.CompilerParams(vmem_limit_bytes=16 * 2**20)
     order = pulse_order.reshape(1, group)
     orders = [order]
-    for apart in range(1, bands):
+    for apart in range(fold, bands, fold):
         orders.append(lax.ppermute(order, "band", [(n, n ^ apart) for n in range(bands)]))
-    vmem = pl.BlockSpec(memory_space=VMEM)
-    params = pltpu.CompilerParams(vmem_limit_bytes=16 * 2**20)
-    f32, bf16 = jnp.float32, jnp.bfloat16
-    shape_of = jax.ShapeDtypeStruct
     views = (
         raw_echoes.reshape(pulses, 2, tiles, LANES).transpose(0, 2, 1, 3),
         matched,
@@ -379,27 +427,22 @@
         order,
     )
     views = [pltpu.with_memory_space_constraint(view, pltpu.HBM) for view in views]
-    prof, high, low, cos_1, sin_1, cos_2, sin_2, orders[0] = pl.pallas_call(
-        functools.partial(compress_kernel, matched.shape[1], local),
-        out_shape=[
-            shape_of((2, 2 * pulses, R), bf16),
-            shape_of((4 * levels, R, R), bf16),
-            shape_of((4 * levels, R, R), bf16),
-            shape_of((pulses // 2, LANES), f32),
-            shape_of((pulses // 2, LANES), f32),
-            shape_of((rows // 2, LANES), f32),
-            shape_of((rows // 2, LANES), f32),
+    compress = pl.pallas_call(
+        functools.partial(compress_kernel, matched.shape[1], local, fold),
+        out_shape=[shape_of((2, rows, R), f32)] * fold
+        + [
+            shape_of((4 * levels, 8, LANES), f32),
+            shape_of((2, 4 * levels, 8, LANES), f32),
+            shape_of((8, LANES), f32),
             shape_of(order.shape, order.dtype),
         ],
         in_specs=[pl.BlockSpec(memory_space=pltpu.HBM)] * 6,
-        out_specs=[vmem] * 8,
+        out_specs=[vmem] * (4 + fold),
         scratch_shapes=[
             VMEM((tiles, 2 * R, LANES), bf16),
             VMEM((tiles, pulses, 2, LANES), bf16),
             VMEM((tiles, 2 * pulses, LANES), bf16),
             VMEM((2, 2 * pulses, R), f32),
-            VMEM((4 * levels, 8, LANES), f32),
-            VMEM((R // 8, 8, LANES), f32),
             VMEM(matched.shape, f32),
             SMEM(views[2].shape, jnp.int32),
             SMEM(views[3].shape, f32),
@@ -413,25 +456,50 @@
         ),
         compiler_params=params,
         name="compress",
-    )(*views)
+    )
+    *shares, starts, edges, angles, orders[0] = compress(*views)
+    for side in range(1, fold):
+        pairs = [(n, n ^ side) for n in range(bands)]
+        shares[side] = lax.ppermute(shares[side], "band", pairs)
+    final_rows = group
+    matrices = pl.pallas_call(
+        functools.partial(matrix_kernel, local, inner),
+        out_shape=[
+            shape_of((4 * levels, R, R), bf16),
+            shape_of((4 * levels, R, R), bf16),
+            shape_of((rows // 2, LANES), f32),
+            shape_of((rows // 2, LANES), f32),
+            shape_of((final_rows // 2, LANES), f32),
+            shape_of((final_rows // 2, LANES), f32),
+        ],
+        in_specs=[vmem] * 3,
+        out_specs=[vmem] * 6,
+        scratch_shapes=[VMEM((R // 8, 8, LANES), f32)],
+        cost_estimate=pl.CostEstimate(
+            flops=400 * levels * R * R, bytes_accessed=16 * levels * R * R, transcendentals=0
+        ),
+        compiler_params=params,
+        name="matrices",
+    )
+    high, low, cos_1, sin_1, cos_2, sin_2 = matrices(starts, edges, angles)
     sent = pl.pallas_call(
-        functools.partial(local_kernel, local, devices),
-        out_shape=shape_of((devices * 2 * kept, R), f32),
-        in_specs=[vmem] * (bands + 5),
+        functools.partial(local_kernel, local, fold),
+        out_shape=shape_of((devices * 2 * per, R), f32),
+        in_specs=[vmem] * (held + fold + 4),
         out_specs=vmem,
-        scratch_shapes=[VMEM((2, 2 * pulses, R), f32)],
+        scratch_shapes=[VMEM((2, 2 * rows, R), f32)],
         compiler_params=params,
         name="levels",
-    )(*orders, prof, high, low, cos_1, sin_1)
+    )(*orders, *shares, high, low, cos_1, sin_1)
     received = lax.all_to_all(
-        sent.reshape(devices, 2 * kept, R), ("aperture", "band"), 0, 0, tiled=True
-    ).reshape(devices * 2 * kept, R)
+        sent.reshape(devices, 2 * per, R), ("aperture", "band"), 0, 0, tiled=True
+    ).reshape(devices * 2 * per, R)
     return pl.pallas_call(
-        functools.partial(final_kernel, local, rest),
-        out_shape=shape_of((rows, R), f32),
+        functools.partial(final_kernel, local, rest, fold),
+        out_shape=shape_of((final_rows, R), f32),
         in_specs=[vmem] * 5,
         out_specs=vmem,
-        scratch_shapes=[VMEM((2, 2 * rows, R), f32), VMEM((2, rows + 16, R), f32)],
+        scratch_shapes=[VMEM((2, 2 * final_rows, R), f32), VMEM((2, final_rows + 16, R), f32)],
         compiler_params=params,
         name="finish",
     )(received, high, low, cos_2, sin_2)
@@ -440,4 +508,5 @@
 def solution(mesh):
     in_specs = (P("aperture", None, "band"), P("aperture", "band", None), P(), P(), P(), P())
     out_specs = P(("band", "aperture"), None)
+
     return jax.shard_map(body, mesh=mesh, in_specs=in_specs, out_specs=out_specs, check_vma=False)

time: 23.5 us -> 23.9 us (1.017)
  waiting for transfers between devices: 0.01 us -> 1.2 us
  blocking collectives: 14.1 us -> 13.6 us
  Pallas kernels: 6.09 us -> 5.85 us
    ppermute x3 -> x1, waiting for transfers between devices: 0.01 us -> 1.2 us  [body(): lax.ppermute(order, 'band', [(n, n ^ apart) for n in range(bands)])]
    ppermute x0 -> x1, starting transfers between devices: none -> 0.57 us  [body(): shares[side] = lax.ppermute(shares[side], 'band', pairs)]
    ppermute x3 -> x1, starting transfers between devices: 3.11 us -> 2.57 us  [body(): lax.ppermute(order, 'band', [(n, n ^ apart) for n in range(bands)])]
    all_to_all x1, blocking collectives: 14.1 us -> 13.6 us  [body(): lax.all_to_all(sent.reshape(devices, 2 * per, R), ('aperture', 'band'), 0...]
    pallas_call x3 -> x4, Pallas kernels: 6.09 us -> 5.85 us  [the longest x1 2.6 us: body(): *shares, starts, edges, angles, orders[0] = compress(*views)]
  transfers between devices with their start and end apart: 3 -> 2, of which waited for: 0 -> 1; matrix products, arithmetic and copies ran while one was open for 0% -> 0% of each run, Pallas kernels for 13% -> 2%
where the time goes in v4:
time: 23.9 us; the launch traced here: 23.8 us
  blocking collectives  13.6 us (57%)
  Pallas kernels  5.85 us (24%)
  starting transfers between devices  3.14 us (13%)
  waiting for transfers between devices  1.2 us (5%)
    all_to_all x1, blocking collectives, body(): lax.all_to_all(sent.reshape(devices, 2 * per, R), ('aperture', 'band'), 0...  13.6 us
    pallas_call x1, Pallas kernels, body(): *shares, starts, edges, angles, orders[0] = compress(*views)  2.6 us
    ppermute x1, starting transfers between devices, body(): lax.ppermute(order, 'band', [(n, n ^ apart) for n in range(bands)])  2.57 us
    pallas_call x1, Pallas kernels, body(): pl.pallas_call(functools.partial(final_kernel, local, rest, fold), out_sh...  1.64 us
    ppermute x1, waiting for transfers between devices, body(): lax.ppermute(order, 'band', [(n, n ^ apart) for n in range(bands)])  1.2 us
    pallas_call x1, Pallas kernels, body(): pl.pallas_call(functools.partial(local_kernel, local, fold), out_shape=sh...  1.13 us
    ppermute x1, starting transfers between devices, body(): shares[side] = lax.ppermute(shares[side], 'band', pairs)  0.57 us
    pallas_call x1, Pallas kernels, body(): high, low, cos_1, sin_1, cos_2, sin_2 = matrices(starts, edges, angles)  0.48 us
  transfers between devices with their start and end apart: 2, of which 1 were waited for; matrix products, arithmetic and copies ran while one was open for 0% of the time, Pallas kernels for 2%

profile of v4, /device:TPU:0, one launch (start us, length us, event | category | flops | bytes accessed | tf_op | source)
XLA Modules:
  0.0 23.8 jit_solution(18043994069122019060)
XLA Ops:
  0.0 2.6 %compress.1 = (f32[2,64,128]{2,1,0:T(8,128)S(1)}, f32[2,64,128]{2,1,0:T(8,128)S(1)}, f32[40,8,128]{2,1,0:T(8,128)S(1)}, f32[2,40,8,128]{3,2,1,0:T(8,128)S(1)}, f...) custom-call(bf16[128,8,2,128]{3,2,1,0:T(2,128)(2,1)} %bitcast.11, f32[2,4096]{1,0:T(2,128)} %refs_1_.1, ...), custom_call_target="tpu_custom_call" | custom-call | flops 134217728 | bytes 524288 | tf_op jit(solution)/shard_map/compress/pallas_call | solution.py:460
  2.6 0.6 %collective-permute-start.1 = (f32[2,64,128]{2,1,0:T(8,128)S(1)}, f32[2,64,128]{2,1,0:T(8,128)S(1)}, u32[]{:S(2)}, u32[]{:S(2)}) collective-permute-start(f32[2,64,128]{2,1,0:T(8,128)S(1)} %get-tuple-element.19), channel_id=1, source_target_pairs={{0,8},{8,0},{16,24},{24,16},{1,9},{9,1},{17,25},{25,17},{2,10},{10... | collective-permute-start | bytes 196616 | tf_op jit(solution)/shard_map/ppermute | solution.py:463
  3.2 2.6 %collective-permute-start = (s32[1,32]{1,0:T(1,128)}, s32[1,32]{1,0:T(1,128)S(1)}, u32[]{:S(2)}, u32[]{:S(2)}) collective-permute-start(s32[1,32]{1,0:T(1,128)} %bitcast.16), channel_id=1, source_target_pairs={{0,16},{8,24},{16,0},{24,8},{1,17},{9,25},{17,1},{25,9},{2,18},{10... | collective-permute-start | bytes 392 | tf_op jit(solution)/shard_map/ppermute | solution.py:420
  5.8 0.5 %matrices.1 = (bf16[40,128,128]{2,1,0:T(8,128)(2,1)S(1)}, bf16[40,128,128]{2,1,0:T(8,128)(2,1)S(1)}, f32[32,128]{1,0:T(8,128)S(1)}, f32[32,128]{1,0:T(8,128)S(1)...) custom-call(f32[40,8,128]{2,1,0:T(8,128)S(1)} %get-tuple-element.20.start_ref, ...), custom_call_target="tpu_custom_call" | custom-call | flops 65536000 | bytes 2621440 | tf_op jit(solution)/shard_map/matrices/pallas_call | solution.py:484
  6.2 1.2 %collective-permute-done.refs_1_ = s32[1,32]{1,0:T(1,128)S(1)} collective-permute-done((s32[1,32]{1,0:T(1,128)}, s32[1,32]{1,0:T(1,128)S(1)}, u32[]{:S(2)}, u32[]{:S(2)}) %collective-permute-start) | collective-permute-done | bytes 160 | tf_op jit(solution)/shard_map/ppermute | solution.py:420
  7.4 0.0 collective-permute-done.1.refs_3_
  7.4 1.1 %levels.1 = f32[128,128]{1,0:T(8,128)S(1)} custom-call(s32[1,32]{1,0:T(1,128)S(1)} %get-tuple-element.17.refs_0_, s32[1,32]{1,0:T(1,128)S(1)} %collective-permute-done.refs_1_, f32[2,64,128]{2,1,0:T(8,128)S(1)} %get-tuple-element.18.refs_2_, f32[2,64,128]{2,1,0:T(8,128)S(1)} %collective-permute-done.1.refs_3_, ...), custom_call_target="tpu_custom_call" | custom-call | tf_op jit(solution)/shard_map/levels/pallas_call | solution.py:485
  8.6 13.6 %all_to_all.5 = f32[32,4,128]{2,1,0:T(4,128)S(1)} all-to-all(f32[32,4,128]{2,1,0:T(4,128)S(1)} %bitcast.10), channel_id=1, replica_groups=mesh['band'=4,'aperture'=8] {'aperture','band'}, dimensions={0} | all-to-all | bytes 131072 | tf_op jit(solution)/shard_map/all_to_all | solution.py:494
  22.1 1.6 %finish.1 = f32[32,128]{1,0:T(8,128)} custom-call(f32[128,128]{1,0:T(8,128)S(1)} %bitcast.9, bf16[40,128,128]{2,1,0:T(8,128)(2,1)S(1)} %get-tuple-element.23.refs_4_.high_ref, bf16[40,128,128]{2,1,0:T(8,128)(2,1)S(1)} %get-tuple-element.24.refs_5_.low_ref, f32[16,128]{1,0:T(8,128)S(1)} %get-tuple-element.27.cos_ref, f32[16,128]{1,0:T(8,128)S(1)} %get-tuple-element.28.sin_ref), custom_call_target="tpu_custom_call" | custom-call | tf_op jit(solution)/shard_map/finish/pallas_call | solution.py:497
Async XLA Ops:
  2.6 4.8 %collective-permute-start.1 = (f32[2,64,128]{2,1,0:T(8,128)S(1)}, f32[2,64,128]{2,1,0:T(8,128)S(1)}, u32[]{:S(2)}, u32[]{:S(2)}) collective-permute-start(f32[2,64,128]{2,1,0:T(8,128)S(1)} %get-tuple-element.19), channel_id=1, source_target_pairs={{0,8},{8,0},{16,24},{24,16},{1,9},{9,1},{17,25},{25,17},{2,10},{10... | collective-permute-start | bytes 196616 | tf_op jit(solution)/shard_map/ppermute | solution.py:463
  3.2 4.3 %collective-permute-start = (s32[1,32]{1,0:T(1,128)}, s32[1,32]{1,0:T(1,128)S(1)}, u32[]{:S(2)}, u32[]{:S(2)}) collective-permute-start(s32[1,32]{1,0:T(1,128)} %bitcast.16), channel_id=1, source_target_pairs={{0,16},{8,24},{16,0},{24,8},{1,17},{9,25},{17,1},{25,9},{2,18},{10... | collective-permute-start | bytes 392 | tf_op jit(solution)/shard_map/ppermute | solution.py:420

commit v5 on v4

--- a/solution.py
+++ b/solution.py
@@ -39,36 +39,38 @@
     )
 
 
-def unit_table(total_freq, start, chunks):
+def unit_rows(total_freq, start, chunks):
     turn = 2.0 * math.pi / total_freq
     rows = -(-chunks // 8) * 8
     f_index = start + iota((rows, LANES), 0) * LANES + iota((rows, LANES), 1)
     angle = f_index.astype(jnp.float32) * turn
-    return jnp.cos(angle), jnp.sin(angle)
-
-
-def make_table(total_freq, start, twiddles, matched_ref, table_ref):
-    chunks = table_ref.shape[0]
-    scale = 1.0 / math.sqrt(total_freq)
-    cos_1, sin_1 = twiddles
+    rows = (jnp.cos(angle), jnp.sin(angle))
     sub = iota((8, LANES), 0)
+    result = []
     for chunk in range(chunks):
-        lanes = pl.ds(pl.multiple_of(start + chunk * LANES, LANES), LANES)
-        power = [
-            jnp.broadcast_to(part[chunk : chunk + 1, :], (8, LANES)) for part in (cos_1, sin_1)
-        ]
-        spec = matched_ref[:, lanes] * scale
-        low = tuple(jnp.broadcast_to(spec[n : n + 1, :], (8, LANES)) for n in range(2))
+        power = [jnp.broadcast_to(part[chunk : chunk + 1, :], (8, LANES)) for part in rows]
+        low = None
         for bit in range(3):
             chosen = (sub >> bit) & 1 == 1
-            low = cmul(low, (jnp.where(chosen, power[0], 1.0), jnp.where(chosen, power[1], 0.0)))
+            factor = (jnp.where(chosen, power[0], 1.0), jnp.where(chosen, power[1], 0.0))
+            low = factor if low is None else cmul(low, factor)
             power = cmul(power, power)
+        result.append((low, power))
+    return result
+
+
+def make_table(total_freq, start, units, matched_ref, table_ref, first):
+    scale = 1.0 / math.sqrt(total_freq)
+    for chunk, (low, power) in enumerate(units):
+        lanes = pl.ds(pl.multiple_of(start + chunk * LANES, LANES), LANES)
+        spec = matched_ref[:, lanes] * scale
+        low = cmul([jnp.broadcast_to(spec[n : n + 1, :], (8, LANES)) for n in range(2)], low)
         block = [jnp.concatenate(parts, axis=0) for parts in zip(low, cmul(low, power))]
         power = cmul(power, power)
         power = [jnp.concatenate([part, part], axis=0) for part in power]
         for begin in range(0, R, 16):
-            table_ref[chunk, begin : begin + 16, :] = block[0].astype(jnp.bfloat16)
-            table_ref[chunk, R + begin : R + begin + 16, :] = block[1].astype(jnp.bfloat16)
+            table_ref[first + chunk, begin : begin + 16, :] = block[0].astype(jnp.bfloat16)
+            table_ref[first + chunk, R + begin : R + begin + 16, :] = block[1].astype(jnp.bfloat16)
             if begin + 16 < R:
                 block = cmul(block, power)
 
@@ -174,78 +176,43 @@
         sin_ref[8 * group : 8 * group + 8, :] = si
 
 
-def compress_kernel(total_freq, local, fold, *refs):
-    echo_ref, matched_hbm, offsets_hbm, fraction_hbm, tilt_hbm, order_hbm = refs[:6]
-    shares, refs = refs[6 : 6 + fold], refs[6 + fold :]
-    start_ref, edge_ref, angle_ref, order_ref = refs[:4]
-    table_ref, echo_buf, line_buf, sum_ref, matched_ref = refs[4:9]
-    offsets_ref, fraction_ref, tilt_ref, sems, line_sems, small_sems = refs[9:]
-    pulses, tiles = echo_ref.shape[:2]
-    freq = tiles * LANES
-    copies = [
-        pltpu.make_async_copy(echo_ref.at[:, n], echo_buf.at[n], sems.at[n]) for n in range(tiles)
-    ]
+def tables_kernel(total_freq, local, inner, fold, echo_hbm, matched_hbm, offsets_hbm, fraction_hbm,
+                  tilt_hbm, order_hbm, echo_ref, order_ref, table_ref, high_ref, low_ref,
+                  cos_ref, sin_ref, cos2_ref, sin2_ref, start_ref, edge_ref, band_ref, angle_ref,
+                  matched_ref, offsets_ref, fraction_ref, tilt_ref, sems):
     pairs = (
         (matched_hbm, matched_ref),
         (offsets_hbm, offsets_ref),
         (fraction_hbm, fraction_ref),
         (tilt_hbm, tilt_ref),
         (order_hbm, order_ref),
+        (echo_hbm, echo_ref),
     )
-    small = [pltpu.make_async_copy(*pair, small_sems.at[n]) for n, pair in enumerate(pairs)]
-    for copy in small + copies:
+    copies = [pltpu.make_async_copy(*pair, sems.at[n]) for n, pair in enumerate(pairs)]
+    for copy in copies:
         copy.start()
-    bands = lax.axis_size("band")
+    tiles = echo_ref.shape[1]
+    freq = tiles * LANES
+    bands, apertures = lax.axis_size("band"), lax.axis_size("aperture")
     band = lax.axis_index("band")
     levels = start_ref.shape[0] // 4
-    twiddles = unit_table(total_freq, band * freq, tiles)
-    for copy in small[1:]:
+    firsts = [(band ^ side) * freq for side in range(fold)]
+    units = [unit_rows(total_freq, first, tiles) for first in firsts]
+    copies[0].wait()
+    for side in range(fold):
+        make_table(total_freq, firsts[side], units[side], matched_ref, table_ref, side * tiles)
+    for copy in copies[1:4]:
         copy.wait()
     build_starts(levels, offsets_ref, fraction_ref, start_ref, edge_ref)
     angle_ref[0:1, :] = build_angles(0, local, tilt_ref)
     angle_ref[1:2, :] = build_angles(local, levels - local, tilt_ref)
-    for copy in copies:
-        copy.wait()
-    copies = [
-        pltpu.make_async_copy(
-            echo_buf.at[n].reshape(2 * pulses, LANES), line_buf.at[n], line_sems.at[n]
-        )
-        for n in range(tiles)
-    ]
-    for copy in copies:
-        copy.start()
-    small[0].wait()
-    make_table(total_freq, band * freq, twiddles, matched_ref, table_ref)
-    for copy in copies:
-        copy.wait()
-    echoes = jnp.concatenate([line_buf[n] for n in range(tiles)], axis=1)
-    dims = (((1,), (1,)), ((), ()))
-    table = jnp.concatenate([table_ref[n] for n in range(tiles)], axis=1)
-    sums = lax.dot_general(echoes, table, dims, preferred_element_type=jnp.float32)
-    sum_ref[0] = sums[:, 0:R]
-    sum_ref[1] = sums[:, R:]
-    group = pulses // bands
-    held = bands // fold
-    for side in range(fold):
-        for member in range(held):
-            first = 2 * group * (member * fold + ((band ^ side) & (fold - 1)))
-            even = pl.ds(pl.multiple_of(first, 8), group, stride=2)
-            odd = pl.ds(first + 1, group, stride=2)
-            re = sum_ref[0, even, :] - sum_ref[1, odd, :]
-            im = sum_ref[1, even, :] + sum_ref[0, odd, :]
-            shares[side][0, member * group : (member + 1) * group, :] = re
-            shares[side][1, member * group : (member + 1) * group, :] = im
-
-
-def matrix_kernel(local, inner, start_ref, edge_ref, angle_ref, high_ref, low_ref,
-                  cos_ref, sin_ref, cos2_ref, sin2_ref, band_ref):
-    bands, apertures = lax.axis_size("band"), lax.axis_size("aperture")
-    levels = start_ref.shape[0] // 4
     build_matrices(start_ref, edge_ref, band_ref, high_ref, low_ref)
     phase_tables(0, local, 0, 0, angle_ref[0:1, :], cos_ref, sin_ref)
-    place = lax.axis_index("aperture") * bands + lax.axis_index("band")
+    place = lax.axis_index("aperture") * bands + band
     tile = bit_reversed(place, (bands * apertures).bit_length() - 1)
     phase_tables(local, levels - local, inner, tile, angle_ref[1:2, :], cos2_ref, sin2_ref)
+    for copy in copies[4:]:
+        copy.wait()
 
 
 def level_step(level, half, source, tables, high_ref, low_ref):
@@ -279,26 +246,60 @@
     return result
 
 
+def product_kernel(fold, *refs):
+    bands = lax.axis_size("band")
+    echoes, (table_ref, prof_ref, sum_ref) = refs[:fold], refs[fold:]
+    pulses, tiles = echoes[0].shape[:2]
+    group = pulses // bands
+    held = bands // fold
+    core = lax.axis_index("band") & (fold - 1)
+    pieces = []
+    for echo_ref in echoes:
+        for n in range(tiles):
+            members = [
+                echo_ref[pl.ds((member * fold + core) * group, group), n].reshape(2 * group, LANES)
+                for member in range(held)
+            ]
+            pieces.append(jnp.concatenate(members, axis=0))
+    table = jnp.concatenate([table_ref[n] for n in range(fold * tiles)], axis=1)
+    sums = lax.dot_general(
+        jnp.concatenate(pieces, axis=1),
+        table,
+        (((1,), (1,)), ((), ())),
+        preferred_element_type=jnp.float32,
+    )
+    sum_ref[0] = sums[:, 0:R]
+    sum_ref[1] = sums[:, R:]
+    rows = group * held
+    even, odd = pl.ds(0, rows, stride=2), pl.ds(1, rows, stride=2)
+    values = (sum_ref[0, even, :] - sum_ref[1, odd, :], sum_ref[1, even, :] + sum_ref[0, odd, :])
+    for part, value in enumerate(values):
+        high, low = halves_of(value)
+        prof_ref[part, 0:rows, :] = high
+        prof_ref[part, rows:, :] = low
+
+
 def local_kernel(count, fold, *refs):
-    devices = lax.axis_size("band") * lax.axis_size("aperture")
-    held = lax.axis_size("band") // fold
-    orders, shares, refs = refs[:held], refs[held : held + fold], refs[held + fold :]
-    high_ref, low_ref, cos_ref, sin_ref, out_ref, image_ref = refs
-    rows = shares[0].shape[1]
+    bands = lax.axis_size("band")
+    devices = bands * lax.axis_size("aperture")
+    held = bands // fold
+    orders, refs = refs[:held], refs[held:]
+    prof_ref, high_ref, low_ref, cos_ref, sin_ref, out_ref, image_ref = refs
+    rows = prof_ref.shape[1] // 2
+    group = rows // held
     half = rows // 2
-    group = rows // held
     me = lax.axis_index("band") // fold
     for apart in range(held):
         start = pl.multiple_of((me ^ apart) * group, group)
         chosen = iota((group, group), 0) == jnp.broadcast_to(orders[apart][...], (group, group))
         chosen = jnp.where(chosen, 1.0, 0.0).astype(jnp.bfloat16)
         twice = jnp.concatenate([chosen, chosen], axis=0)
-        parts = []
-        for part in range(2):
-            value = shares[0][part, pl.ds(start, group), :]
-            for share in shares[1:]:
-                value = value + share[part, pl.ds(start, group), :]
-            parts.append(jnp.concatenate(halves_of(value), axis=0))
+        parts = [
+            jnp.concatenate(
+                [prof_ref[part, pl.ds(side + start, group), :] for side in (0, rows)], axis=0
+            )
+            for part in range(2)
+        ]
         moved = lax.dot_general(
             twice,
             jnp.concatenate(parts, axis=1),
@@ -418,8 +419,15 @@
     orders = [order]
     for apart in range(fold, bands, fold):
         orders.append(lax.ppermute(order, "band", [(n, n ^ apart) for n in range(bands)]))
+    echo_parts = [raw_echoes]
+    for side in range(1, fold):
+        pairs = [(n, n ^ side) for n in range(bands)]
+        echo_parts.append(lax.ppermute(raw_echoes, "band", pairs))
+    echoes = [
+        part.reshape(pulses, 2, tiles, LANES).transpose(0, 2, 1, 3) for part in echo_parts
+    ]
     views = (
-        raw_echoes.reshape(pulses, 2, tiles, LANES).transpose(0, 2, 1, 3),
+        echoes[0],
         matched,
         offsets.transpose(1, 2, 3, 0),
         fraction.transpose(1, 2, 0),
@@ -427,79 +435,70 @@
         order,
     )
     views = [pltpu.with_memory_space_constraint(view, pltpu.HBM) for view in views]
-    compress = pl.pallas_call(
-        functools.partial(compress_kernel, matched.shape[1], local, fold),
-        out_shape=[shape_of((2, rows, R), f32)] * fold
-        + [
-            shape_of((4 * levels, 8, LANES), f32),
-            shape_of((2, 4 * levels, 8, LANES), f32),
-            shape_of((8, LANES), f32),
+    tables = pl.pallas_call(
+        functools.partial(tables_kernel, matched.shape[1], local, inner, fold),
+        out_shape=[
+            shape_of(echoes[0].shape, bf16),
             shape_of(order.shape, order.dtype),
+            shape_of((fold * tiles, 2 * R, LANES), bf16),
+            shape_of((4 * levels, R, R), bf16),
+            shape_of((4 * levels, R, R), bf16),
+            shape_of((rows // 2, LANES), f32),
+            shape_of((rows // 2, LANES), f32),
+            shape_of((group // 2, LANES), f32),
+            shape_of((group // 2, LANES), f32),
         ],
         in_specs=[pl.BlockSpec(memory_space=pltpu.HBM)] * 6,
-        out_specs=[vmem] * (4 + fold),
+        out_specs=[vmem] * 9,
         scratch_shapes=[
-            VMEM((tiles, 2 * R, LANES), bf16),
-            VMEM((tiles, pulses, 2, LANES), bf16),
-            VMEM((tiles, 2 * pulses, LANES), bf16),
-            VMEM((2, 2 * pulses, R), f32),
+            VMEM((4 * levels, 8, LANES), f32),
+            VMEM((2, 4 * levels, 8, LANES), f32),
+            VMEM((R // 8, 8, LANES), f32),
+            VMEM((8, LANES), f32),
             VMEM(matched.shape, f32),
             SMEM(views[2].shape, jnp.int32),
             SMEM(views[3].shape, f32),
             SMEM(views[4].shape, f32),
-            pltpu.SemaphoreType.DMA((tiles,)),
-            pltpu.SemaphoreType.DMA((tiles,)),
-            pltpu.SemaphoreType.DMA((5,)),
+            pltpu.SemaphoreType.DMA((6,)),
         ],
+        cost_estimate=pl.CostEstimate(
+            flops=400 * levels * R * R, bytes_accessed=16 * levels * R * R, transcendentals=0
+        ),
+        compiler_params=params,
+        name="tables",
+    )
+    echoes[0], orders[0], table, high, low, cos_1, sin_1, cos_2, sin_2 = tables(*views)
+    product = pl.pallas_call(
+        functools.partial(product_kernel, fold),
+        out_shape=shape_of((2, 2 * rows, R), bf16),
+        in_specs=[vmem] * (fold + 1),
+        out_specs=vmem,
+        scratch_shapes=[VMEM((2, 2 * rows, R), f32)],
         cost_estimate=pl.CostEstimate(
             flops=8 * pulses * freq * R, bytes_accessed=4 * pulses * freq, transcendentals=0
         ),
         compiler_params=params,
-        name="compress",
+        name="product",
     )
-    *shares, starts, edges, angles, orders[0] = compress(*views)
-    for side in range(1, fold):
-        pairs = [(n, n ^ side) for n in range(bands)]
-        shares[side] = lax.ppermute(shares[side], "band", pairs)
-    final_rows = group
-    matrices = pl.pallas_call(
-        functools.partial(matrix_kernel, local, inner),
-        out_shape=[
-            shape_of((4 * levels, R, R), bf16),
-            shape_of((4 * levels, R, R), bf16),
-            shape_of((rows // 2, LANES), f32),
-            shape_of((rows // 2, LANES), f32),
-            shape_of((final_rows // 2, LANES), f32),
-            shape_of((final_rows // 2, LANES), f32),
-        ],
-        in_specs=[vmem] * 3,
-        out_specs=[vmem] * 6,
-        scratch_shapes=[VMEM((R // 8, 8, LANES), f32)],
-        cost_estimate=pl.CostEstimate(
-            flops=400 * levels * R * R, bytes_accessed=16 * levels * R * R, transcendentals=0
-        ),
-        compiler_params=params,
-        name="matrices",
-    )
-    high, low, cos_1, sin_1, cos_2, sin_2 = matrices(starts, edges, angles)
+    prof = product(*echoes, table)
     sent = pl.pallas_call(
         functools.partial(local_kernel, local, fold),
         out_shape=shape_of((devices * 2 * per, R), f32),
-        in_specs=[vmem] * (held + fold + 4),
+        in_specs=[vmem] * (held + 5),
         out_specs=vmem,
         scratch_shapes=[VMEM((2, 2 * rows, R), f32)],
         compiler_params=params,
         name="levels",
-    )(*orders, *shares, high, low, cos_1, sin_1)
+    )(*orders, prof, high, low, cos_1, sin_1)
     received = lax.all_to_all(
         sent.reshape(devices, 2 * per, R), ("aperture", "band"), 0, 0, tiled=True
     ).reshape(devices * 2 * per, R)
     return pl.pallas_call(
         functools.partial(final_kernel, local, rest, fold),
-        out_shape=shape_of((final_rows, R), f32),
+        out_shape=shape_of((group, R), f32),
         in_specs=[vmem] * 5,
         out_specs=vmem,
-        scratch_shapes=[VMEM((2, 2 * final_rows, R), f32), VMEM((2, final_rows + 16, R), f32)],
+        scratch_shapes=[VMEM((2, 2 * group, R), f32), VMEM((2, group + 16, R), f32)],
         compiler_params=params,
         name="finish",
     )(received, high, low, cos_2, sin_2)

time: 23.9 us -> 21.2 us (0.89)
  waiting for transfers between devices: 1.2 us -> 0.01 us
  Pallas kernels: 5.85 us -> 5.05 us
  blocking collectives: 13.6 us -> 12.9 us
    ppermute x1, waiting for transfers between devices: 1.2 us -> 0.01 us  [body(): lax.ppermute(order, 'band', [(n, n ^ apart) for n in range(bands)])]
    pallas_call x2, Pallas kernels: 3.08 us -> 2.28 us  [the longest x1 1.8 us: body(): tables(*views)]
    all_to_all x1, blocking collectives: 13.6 us -> 12.9 us  [body(): lax.all_to_all(sent.reshape(devices, 2 * per, R), ('aperture', 'band'), 0...]
  transfers between devices with their start and end apart: 2 -> 2, of which waited for: 1 -> 0; matrix products, arithmetic and copies ran while one was open for 0% -> 0% of each run, Pallas kernels for 2% -> 11%
where the time goes in v5:
time: 21.2 us; the launch traced here: 21 us
  blocking collectives  12.9 us (61%)
  Pallas kernels  5.05 us (24%)
  starting transfers between devices  3 us (14%)
    all_to_all x1, blocking collectives, body(): lax.all_to_all(sent.reshape(devices, 2 * per, R), ('aperture', 'band'), 0...  12.9 us
    ppermute x1, starting transfers between devices, body(): lax.ppermute(order, 'band', [(n, n ^ apart) for n in range(bands)])  2.51 us
    pallas_call x1, Pallas kernels, body(): tables(*views)  1.8 us
    pallas_call x1, Pallas kernels, body(): pl.pallas_call(functools.partial(final_kernel, local, rest, fold), out_sh...  1.64 us
    pallas_call x1, Pallas kernels, body(): pl.pallas_call(functools.partial(local_kernel, local, fold), out_shape=sh...  1.13 us
    ppermute x1, starting transfers between devices, body(): echo_parts.append(lax.ppermute(raw_echoes, 'band', pairs))  0.49 us
    pallas_call x1, Pallas kernels, body(): prof = product(*echoes, table)  0.48 us
  transfers between devices with their start and end apart: 2, of which 0 were waited for; matrix products, arithmetic and copies ran while one was open for 0% of the time, Pallas kernels for 11%

profile of v5, /device:TPU:0, one launch (start us, length us, event | category | flops | bytes accessed | tf_op | source)
XLA Modules:
  0.0 21.0 jit_solution(4516825465711641498)
XLA Ops:
  0.0 0.5 %collective-permute-start.1 = (bf16[128,2,1024]{2,1,0:T(2,128)(2,1)}, bf16[128,2,1024]{2,1,0:T(2,128)(2,1)S(1)}, u32[]{:S(2)}, u32[]{:S(2)}) collective-permute-start(bf16[128,2,1024]{2,1,0:T(2,128)(2,1)} %param.6), channel_id=1, source_target_pairs={{0,8},{8,0},{16,24},{24,16},{1,9},{9,1},{17,25},{25,17},{2,10},{10... | collective-permute-start | bytes 1572872 | tf_op jit(solution)/shard_map/ppermute | solution.py:425
  0.5 2.5 %collective-permute-start = (s32[1,32]{1,0:T(1,128)}, s32[1,32]{1,0:T(1,128)S(1)}, u32[]{:S(2)}, u32[]{:S(2)}) collective-permute-start(s32[1,32]{1,0:T(1,128)} %bitcast.19), channel_id=1, source_target_pairs={{0,16},{8,24},{16,0},{24,8},{1,17},{9,25},{17,1},{25,9},{2,18},{10... | collective-permute-start | bytes 392 | tf_op jit(solution)/shard_map/ppermute | solution.py:421
  3.0 1.8 %tables.1 = (bf16[128,8,2,128]{3,2,1,0:T(2,128)(2,1)S(1)}, s32[1,32]{1,0:T(1,128)S(1)}, bf16[16,256,128]{2,1,0:T(8,128)(2,1)S(1)}, bf16[40,128,128]{2,1,0:T(8,12...) custom-call(bf16[128,8,2,128]{3,2,1,0:T(2,128)(2,1)} %bitcast.15, ...), custom_call_target="tpu_custom_call" | custom-call | flops 65536000 | bytes 2621440 | tf_op jit(solution)/shard_map/tables/pallas_call | solution.py:470
  4.8 0.0 collective-permute-done.1
  4.8 0.5 %product.1.refs_2_ = bf16[2,128,128]{2,1,0:T(8,128)(2,1)S(1)} custom-call(bf16[128,8,2,128]{3,2,1,0:T(2,128)(2,1)S(1)} %get-tuple-element.15.refs_0_, bf16[128,8,2,128]{3,2,1,0:T(2,128)(2,1)S(1)} %bitcast.12, bf16[16,256,128]{2,1,0:T(8,128)(2,1)S(1)} %get-tuple-element.16.refs_2_), custom_call_target="tpu_custom_call" | custom-call | flops 134217728 | bytes 524288 | tf_op jit(solution)/shard_map/product/pallas_call | solution.py:483
  5.3 0.0 collective-permute-done.refs_1_
  5.3 1.1 %levels.1 = f32[128,128]{1,0:T(8,128)S(1)} custom-call(s32[1,32]{1,0:T(1,128)S(1)} %get-tuple-element.14.refs_0_, s32[1,32]{1,0:T(1,128)S(1)} %collective-permute-done.refs_1_, bf16[2,128,128]{2,1,0:T(8,128)(2,1)S(1)} %product.1.refs_2_, bf16[40,128,128]{2,1,0:T(8,128)(2,1)S(1)} %get-tuple-element.17.refs_3_.high_ref, ...), custom_call_target="tpu_custom_call" | custom-call | tf_op jit(solution)/shard_map/levels/pallas_call | solution.py:484
  6.4 12.9 %all_to_all.5 = f32[32,4,128]{2,1,0:T(4,128)S(1)} all-to-all(f32[32,4,128]{2,1,0:T(4,128)S(1)} %bitcast.14), channel_id=1, replica_groups=mesh['band'=4,'aperture'=8] {'aperture','band'}, dimensions={0} | all-to-all | bytes 131072 | tf_op jit(solution)/shard_map/all_to_all | solution.py:493
  19.4 1.6 %finish.1 = f32[32,128]{1,0:T(8,128)} custom-call(f32[128,128]{1,0:T(8,128)S(1)} %bitcast.13, bf16[40,128,128]{2,1,0:T(8,128)(2,1)S(1)} %get-tuple-element.17.refs_3_.high_ref, bf16[40,128,128]{2,1,0:T(8,128)(2,1)S(1)} %get-tuple-element.18.refs_4_.low_ref, f32[16,128]{1,0:T(8,128)S(1)} %get-tuple-element.21.cos_ref, f32[16,128]{1,0:T(8,128)S(1)} %get-tuple-element.22.sin_ref), custom_call_target="tpu_custom_call" | custom-call | tf_op jit(solution)/shard_map/finish/pallas_call | solution.py:496
Async XLA Ops:
  0.0 4.8 %collective-permute-start.1 = (bf16[128,2,1024]{2,1,0:T(2,128)(2,1)}, bf16[128,2,1024]{2,1,0:T(2,128)(2,1)S(1)}, u32[]{:S(2)}, u32[]{:S(2)}) collective-permute-start(bf16[128,2,1024]{2,1,0:T(2,128)(2,1)} %param.6), channel_id=1, source_target_pairs={{0,8},{8,0},{16,24},{24,16},{1,9},{9,1},{17,25},{25,17},{2,10},{10... | collective-permute-start | bytes 1572872 | tf_op jit(solution)/shard_map/ppermute | solution.py:425
  0.5 4.8 %collective-permute-start = (s32[1,32]{1,0:T(1,128)}, s32[1,32]{1,0:T(1,128)S(1)}, u32[]{:S(2)}, u32[]{:S(2)}) collective-permute-start(s32[1,32]{1,0:T(1,128)} %bitcast.19), channel_id=1, source_target_pairs={{0,16},{8,24},{16,0},{24,8},{1,17},{9,25},{17,1},{25,9},{2,18},{10... | collective-permute-start | bytes 392 | tf_op jit(solution)/shard_map/ppermute | solution.py:421

commit v6 on v5

--- a/solution.py
+++ b/solution.py
@@ -215,20 +215,26 @@
         copy.wait()
 
 
-def level_step(level, half, source, tables, high_ref, low_ref):
+def interpolated(held, at, high_ref, low_ref):
+    high, low = halves_of(held)
+    m_high, m_low = (
+        jnp.concatenate([ref[at], ref[at + 1]], axis=1) for ref in (high_ref, low_ref)
+    )
+    dot = functools.partial(jnp.dot, preferred_element_type=jnp.float32)
+    both = jnp.concatenate([high, low], axis=1)
+    return dot(both, jnp.concatenate([m_high, m_high], axis=0)) + dot(high, m_low)
+
+
+def children_of(source, half):
+    return [source[pl.ds(child, 2 * half, stride=2), :] for child in range(2)]
+
+
+def level_step(level, half, children, tables, high_ref, low_ref):
     cos_ref, sin_ref = tables
-    products = []
-    for child in range(2):
-        held = source[pl.ds(child, 2 * half, stride=2), :]
-        high, low = halves_of(held)
-        at = 4 * level + 2 * child
-        m_high, m_low = (
-            jnp.concatenate([ref[at], ref[at + 1]], axis=1) for ref in (high_ref, low_ref)
-        )
-        dot = functools.partial(jnp.dot, preferred_element_type=jnp.float32)
-        both = jnp.concatenate([high, low], axis=1)
-        m_both = jnp.concatenate([m_high, m_high], axis=0)
-        products.append(dot(both, m_both) + dot(high, m_low))
+    products = [
+        interpolated(held, 4 * level + 2 * child, high_ref, low_ref)
+        for child, held in enumerate(children)
+    ]
     result = []
     for parity in range(2):
         re = im = None
@@ -248,7 +254,8 @@
 
 def product_kernel(fold, *refs):
     bands = lax.axis_size("band")
-    echoes, (table_ref, prof_ref, sum_ref) = refs[:fold], refs[fold:]
+    echoes, refs = refs[:fold], refs[fold:]
+    table_ref, high_ref, low_ref, cos_ref, sin_ref, prof_ref, sum_ref = refs
     pulses, tiles = echoes[0].shape[:2]
     group = pulses // bands
     held = bands // fold
@@ -273,10 +280,21 @@
     rows = group * held
     even, odd = pl.ds(0, rows, stride=2), pl.ds(1, rows, stride=2)
     values = (sum_ref[0, even, :] - sum_ref[1, odd, :], sum_ref[1, even, :] + sum_ref[0, odd, :])
-    for part, value in enumerate(values):
-        high, low = halves_of(value)
-        prof_ref[part, 0:rows, :] = high
-        prof_ref[part, rows:, :] = low
+    both = jnp.concatenate(values, axis=0)
+    for child in range(2):
+        result = interpolated(both, 2 * child, high_ref, low_ref)
+        for parity in range(2):
+            entry = 2 * child + parity
+            phase = (cos_ref[0:1, entry : entry + 1], sin_ref[0:1, entry : entry + 1])
+            column = slice(parity * R, (parity + 1) * R)
+            turned = cmul((result[0:rows, column], result[rows:, column]), phase)
+            for part, value in enumerate(turned):
+                for side, half in enumerate(halves_of(value)):
+                    at = (2 * side + child) * group
+                    for member in range(held):
+                        prof_ref[parity, part, member, at : at + group, :] = half[
+                            member * group : (member + 1) * group
+                        ]
 
 
 def local_kernel(count, fold, *refs):
@@ -284,33 +302,42 @@
     devices = bands * lax.axis_size("aperture")
     held = bands // fold
     orders, refs = refs[:held], refs[held:]
-    prof_ref, high_ref, low_ref, cos_ref, sin_ref, out_ref, image_ref = refs
-    rows = prof_ref.shape[1] // 2
-    group = rows // held
+    prof_ref, high_ref, low_ref, cos_ref, sin_ref, out_ref, image_ref, pick_ref = refs
+    group = prof_ref.shape[3] // 4
+    rows = group * held
     half = rows // 2
     me = lax.axis_index("band") // fold
     for apart in range(held):
-        start = pl.multiple_of((me ^ apart) * group, group)
-        chosen = iota((group, group), 0) == jnp.broadcast_to(orders[apart][...], (group, group))
-        chosen = jnp.where(chosen, 1.0, 0.0).astype(jnp.bfloat16)
-        twice = jnp.concatenate([chosen, chosen], axis=0)
-        parts = [
-            jnp.concatenate(
-                [prof_ref[part, pl.ds(side + start, group), :] for side in (0, rows)], axis=0
+        member = me ^ apart
+        start = pl.multiple_of(member * group, group)
+        match = iota((group, group), 0) == jnp.broadcast_to(orders[apart][...], (group, group))
+        lane = iota((group, group), 1)
+        chosen = [jnp.where(match & (lane & 1 == child), 1.0, 0.0) for child in range(2)]
+        chosen = jnp.concatenate(chosen + chosen, axis=0).astype(jnp.bfloat16)
+        for parity in range(2):
+            moved = lax.dot_general(
+                chosen,
+                jnp.concatenate([prof_ref[parity, part, member] for part in range(2)], axis=1),
+                (((0,), (0,)), ((), ())),
+                preferred_element_type=jnp.float32,
             )
-            for part in range(2)
-        ]
-        moved = lax.dot_general(
-            twice,
-            jnp.concatenate(parts, axis=1),
-            (((0,), (0,)), ((), ())),
-            preferred_element_type=jnp.float32,
-        )
-        image_ref[0, pl.ds(start, group), :] = moved[:, 0:R]
-        image_ref[0, pl.ds(rows + start, group), :] = moved[:, R:]
-    for level in range(count):
+            for part in range(2):
+                pick_ref[parity, part, pl.ds(start, group), :] = moved[:, part * R : (part + 1) * R]
+    for level in range(1, count):
         source, target = image_ref.at[level % 2], image_ref.at[(level + 1) % 2]
-        result = level_step(level, half, source, (cos_ref, sin_ref), high_ref, low_ref)
+        if level == 1:
+            children = []
+            for child in range(0, 4, 2):
+                parts = [
+                    pick_ref[parity, part, pl.ds(child, rows // 4, stride=4), :]
+                    + pick_ref[parity, part, pl.ds(child + 1, rows // 4, stride=4), :]
+                    for part in range(2)
+                    for parity in range(2)
+                ]
+                children.append(jnp.concatenate(parts, axis=0))
+        else:
+            children = children_of(source, half)
+        result = level_step(level, half, children, (cos_ref, sin_ref), high_ref, low_ref)
         for parity in range(2):
             for part in range(2):
                 target[pl.ds(part * rows + parity * half, half), :] = result[parity][part]
@@ -366,7 +393,8 @@
                 image_ref[0, place, :] = total
     for level in range(count):
         source, target = image_ref.at[level % 2], image_ref.at[(level + 1) % 2]
-        result = level_step(level, half, source, (cos_ref, sin_ref), high_ref, low_ref)
+        children = children_of(source, half)
+        result = level_step(level, half, children, (cos_ref, sin_ref), high_ref, low_ref)
         for parity in range(2):
             for part in range(2):
                 target[pl.ds(part * rows + parity * half, half), :] = result[parity][part]
@@ -470,8 +498,8 @@
     echoes[0], orders[0], table, high, low, cos_1, sin_1, cos_2, sin_2 = tables(*views)
     product = pl.pallas_call(
         functools.partial(product_kernel, fold),
-        out_shape=shape_of((2, 2 * rows, R), bf16),
-        in_specs=[vmem] * (fold + 1),
+        out_shape=shape_of((2, 2, held, 4 * group, R), bf16),
+        in_specs=[vmem] * (fold + 5),
         out_specs=vmem,
         scratch_shapes=[VMEM((2, 2 * rows, R), f32)],
         cost_estimate=pl.CostEstimate(
@@ -480,13 +508,13 @@
         compiler_params=params,
         name="product",
     )
-    prof = product(*echoes, table)
+    prof = product(*echoes, table, high, low, cos_1, sin_1)
     sent = pl.pallas_call(
         functools.partial(local_kernel, local, fold),
         out_shape=shape_of((devices * 2 * per, R), f32),
         in_specs=[vmem] * (held + 5),
         out_specs=vmem,
-        scratch_shapes=[VMEM((2, 2 * rows, R), f32)],
+        scratch_shapes=[VMEM((2, 2 * rows, R), f32), VMEM((2, 2, rows, R), f32)],
         compiler_params=params,
         name="levels",
     )(*orders, prof, high, low, cos_1, sin_1)

time: 21.2 us -> 21 us (level)
  blocking collectives: 12.9 us -> 12.6 us
    all_to_all x1, blocking collectives: 12.9 us -> 12.6 us  [body(): lax.all_to_all(sent.reshape(devices, 2 * per, R), ('aperture', 'band'), 0...]
    pallas_call x1, Pallas kernels: 0.48 us -> 0.8 us  [body(): prof = product(*echoes, table, high, low, cos_1, sin_1)]
  transfers between devices with their start and end apart: 2 -> 2, of which waited for: 0 -> 0; matrix products, arithmetic and copies ran while one was open for 0% -> 0% of each run, Pallas kernels for 11% -> 12%
where the time goes in v6:
time: 21 us; the launch traced here: 20.8 us
  blocking collectives  12.6 us (60%)
  Pallas kernels  5.19 us (25%)
  starting transfers between devices  3 us (14%)
    all_to_all x1, blocking collectives, body(): lax.all_to_all(sent.reshape(devices, 2 * per, R), ('aperture', 'band'), 0...  12.6 us
    ppermute x1, starting transfers between devices, body(): lax.ppermute(order, 'band', [(n, n ^ apart) for n in range(bands)])  2.51 us
    pallas_call x1, Pallas kernels, body(): tables(*views)  1.8 us
    pallas_call x1, Pallas kernels, body(): pl.pallas_call(functools.partial(final_kernel, local, rest, fold), out_sh...  1.63 us
    pallas_call x1, Pallas kernels, body(): pl.pallas_call(functools.partial(local_kernel, local, fold), out_shape=sh...  0.96 us
    pallas_call x1, Pallas kernels, body(): prof = product(*echoes, table, high, low, cos_1, sin_1)  0.8 us
    ppermute x1, starting transfers between devices, body(): echo_parts.append(lax.ppermute(raw_echoes, 'band', pairs))  0.49 us
  transfers between devices with their start and end apart: 2, of which 0 were waited for; matrix products, arithmetic and copies ran while one was open for 0% of the time, Pallas kernels for 12%

profile of v6, /device:TPU:0, one launch (start us, length us, event | category | flops | bytes accessed | tf_op | source)
XLA Modules:
  0.0 20.8 jit_solution(2240446172321363477)
XLA Ops:
  0.0 0.5 %collective-permute-start.1 = (bf16[128,2,1024]{2,1,0:T(2,128)(2,1)}, bf16[128,2,1024]{2,1,0:T(2,128)(2,1)S(1)}, u32[]{:S(2)}, u32[]{:S(2)}) collective-permute-start(bf16[128,2,1024]{2,1,0:T(2,128)(2,1)} %param.6), channel_id=1, source_target_pairs={{0,8},{8,0},{16,24},{24,16},{1,9},{9,1},{17,25},{25,17},{2,10},{10... | collective-permute-start | bytes 1572872 | tf_op jit(solution)/shard_map/ppermute | solution.py:453
  0.5 2.5 %collective-permute-start = (s32[1,32]{1,0:T(1,128)}, s32[1,32]{1,0:T(1,128)S(1)}, u32[]{:S(2)}, u32[]{:S(2)}) collective-permute-start(s32[1,32]{1,0:T(1,128)} %bitcast.19), channel_id=1, source_target_pairs={{0,16},{8,24},{16,0},{24,8},{1,17},{9,25},{17,1},{25,9},{2,18},{10... | collective-permute-start | bytes 392 | tf_op jit(solution)/shard_map/ppermute | solution.py:449
  3.0 1.8 %tables.1 = (bf16[128,8,2,128]{3,2,1,0:T(2,128)(2,1)S(1)}, s32[1,32]{1,0:T(1,128)S(1)}, bf16[16,256,128]{2,1,0:T(8,128)(2,1)S(1)}, bf16[40,128,128]{2,1,0:T(8,12...) custom-call(bf16[128,8,2,128]{3,2,1,0:T(2,128)(2,1)} %bitcast.15, ...), custom_call_target="tpu_custom_call" | custom-call | flops 65536000 | bytes 2621440 | tf_op jit(solution)/shard_map/tables/pallas_call | solution.py:498
  4.8 0.0 collective-permute-done.1
  4.8 0.8 %product.1.refs_2_ = bf16[2,2,2,128,128]{4,3,2,1,0:T(8,128)(2,1)S(1)} custom-call(bf16[128,8,2,128]{3,2,1,0:T(2,128)(2,1)S(1)} %get-tuple-element.15.refs_0_, bf16[128,8,2,128]{3,2,1,0:T(2,128)(2,1)S(1)} %bitcast.12, bf16[16,256,128]{2,1,0:T(8,128)(2,1)S(1)} %get-tuple-element.16.refs_2_, bf16[40,128,128]{2,1,0:T(8,128)(2,1)S(1)} %get-tuple-element.17.refs_3_.high_ref, ...), custom_call_target="tpu_custom_call" | custom-call | flops 134217728 | bytes 524288 | tf_op jit(solution)/shard_map/product/pallas_call | solution.py:511
  5.6 0.0 collective-permute-done.refs_1_
  5.6 1.0 %levels.1 = f32[128,128]{1,0:T(8,128)S(1)} custom-call(s32[1,32]{1,0:T(1,128)S(1)} %get-tuple-element.14.refs_0_, s32[1,32]{1,0:T(1,128)S(1)} %collective-permute-done.refs_1_, bf16[2,2,2,128,128]{4,3,2,1,0:T(8,128)(2,1)S(1)} %product.1.refs_2_, bf16[40,128,128]{2,1,0:T(8,128)(2,1)S(1)} %get-tuple-element.17.refs_3_.high_ref, ...), custom_call_target="tpu_custom_call" | custom-call | tf_op jit(solution)/shard_map/levels/pallas_call | solution.py:512
  6.6 12.6 %all_to_all.5 = f32[32,4,128]{2,1,0:T(4,128)S(1)} all-to-all(f32[32,4,128]{2,1,0:T(4,128)S(1)} %bitcast.14), channel_id=1, replica_groups=mesh['band'=4,'aperture'=8] {'aperture','band'}, dimensions={0} | all-to-all | bytes 131072 | tf_op jit(solution)/shard_map/all_to_all | solution.py:521
  19.2 1.6 %finish.1 = f32[32,128]{1,0:T(8,128)} custom-call(f32[128,128]{1,0:T(8,128)S(1)} %bitcast.13, bf16[40,128,128]{2,1,0:T(8,128)(2,1)S(1)} %get-tuple-element.17.refs_3_.high_ref, bf16[40,128,128]{2,1,0:T(8,128)(2,1)S(1)} %get-tuple-element.18.refs_4_.low_ref, f32[16,128]{1,0:T(8,128)S(1)} %get-tuple-element.21.cos_ref, f32[16,128]{1,0:T(8,128)S(1)} %get-tuple-element.22.sin_ref), custom_call_target="tpu_custom_call" | custom-call | tf_op jit(solution)/shard_map/finish/pallas_call | solution.py:524
Async XLA Ops:
  0.0 4.8 %collective-permute-start.1 = (bf16[128,2,1024]{2,1,0:T(2,128)(2,1)}, bf16[128,2,1024]{2,1,0:T(2,128)(2,1)S(1)}, u32[]{:S(2)}, u32[]{:S(2)}) collective-permute-start(bf16[128,2,1024]{2,1,0:T(2,128)(2,1)} %param.6), channel_id=1, source_target_pairs={{0,8},{8,0},{16,24},{24,16},{1,9},{9,1},{17,25},{25,17},{2,10},{10... | collective-permute-start | bytes 1572872 | tf_op jit(solution)/shard_map/ppermute | solution.py:453
  0.5 5.1 %collective-permute-start = (s32[1,32]{1,0:T(1,128)}, s32[1,32]{1,0:T(1,128)S(1)}, u32[]{:S(2)}, u32[]{:S(2)}) collective-permute-start(s32[1,32]{1,0:T(1,128)} %bitcast.19), channel_id=1, source_target_pairs={{0,16},{8,24},{16,0},{24,8},{1,17},{9,25},{17,1},{25,9},{2,18},{10... | collective-permute-start | bytes 392 | tf_op jit(solution)/shard_map/ppermute | solution.py:449

commit v7 on v6

--- a/solution.py
+++ b/solution.py
@@ -221,8 +221,12 @@
         jnp.concatenate([ref[at], ref[at + 1]], axis=1) for ref in (high_ref, low_ref)
     )
     dot = functools.partial(jnp.dot, preferred_element_type=jnp.float32)
-    both = jnp.concatenate([high, low], axis=1)
-    return dot(both, jnp.concatenate([m_high, m_high], axis=0)) + dot(high, m_low)
+    rows = held.shape[0]
+    if 4 * rows <= R:
+        stacked = dot(jnp.concatenate([high, low], axis=0), m_high)
+        return (stacked[:rows] + stacked[rows:]) + dot(high, m_low)
+    left = jnp.concatenate([high, low, high], axis=1)
+    return dot(left, jnp.concatenate([m_high, m_high, m_low], axis=0))
 
 
 def children_of(source, half):

time: 21 us -> 20.9 us (level)
  transfers between devices with their start and end apart: 2 -> 2, of which waited for: 0 -> 0; matrix products, arithmetic and copies ran while one was open for 0% -> 0% of each run, Pallas kernels for 12% -> 13%
where the time goes in v7:
time: 20.9 us; the launch traced here: 20.7 us
  blocking collectives  12.6 us (60%)
  Pallas kernels  5.08 us (24%)
  starting transfers between devices  3 us (14%)
    all_to_all x1, blocking collectives, body(): lax.all_to_all(sent.reshape(devices, 2 * per, R), ('aperture', 'band'), 0...  12.6 us
    ppermute x1, starting transfers between devices, body(): lax.ppermute(order, 'band', [(n, n ^ apart) for n in range(bands)])  2.51 us
    pallas_call x1, Pallas kernels, body(): tables(*views)  1.8 us
    pallas_call x1, Pallas kernels, body(): pl.pallas_call(functools.partial(final_kernel, local, rest, fold), out_sh...  1.57 us
    pallas_call x1, Pallas kernels, body(): pl.pallas_call(functools.partial(local_kernel, local, fold), out_shape=sh...  0.91 us
    pallas_call x1, Pallas kernels, body(): prof = product(*echoes, table, high, low, cos_1, sin_1)  0.8 us
    ppermute x1, starting transfers between devices, body(): echo_parts.append(lax.ppermute(raw_echoes, 'band', pairs))  0.49 us
  transfers between devices with their start and end apart: 2, of which 0 were waited for; matrix products, arithmetic and copies ran while one was open for 0% of the time, Pallas kernels for 13%

profile of v7, /device:TPU:0, one launch (start us, length us, event | category | flops | bytes accessed | tf_op | source)
XLA Modules:
  0.0 20.7 jit_solution(3784360191947037502)
XLA Ops:
  0.0 0.5 %collective-permute-start.1 = (bf16[128,2,1024]{2,1,0:T(2,128)(2,1)}, bf16[128,2,1024]{2,1,0:T(2,128)(2,1)S(1)}, u32[]{:S(2)}, u32[]{:S(2)}) collective-permute-start(bf16[128,2,1024]{2,1,0:T(2,128)(2,1)} %param.6), channel_id=1, source_target_pairs={{0,8},{8,0},{16,24},{24,16},{1,9},{9,1},{17,25},{25,17},{2,10},{10... | collective-permute-start | bytes 1572872 | tf_op jit(solution)/shard_map/ppermute | solution.py:457
  0.5 2.5 %collective-permute-start = (s32[1,32]{1,0:T(1,128)}, s32[1,32]{1,0:T(1,128)S(1)}, u32[]{:S(2)}, u32[]{:S(2)}) collective-permute-start(s32[1,32]{1,0:T(1,128)} %bitcast.19), channel_id=1, source_target_pairs={{0,16},{8,24},{16,0},{24,8},{1,17},{9,25},{17,1},{25,9},{2,18},{10... | collective-permute-start | bytes 392 | tf_op jit(solution)/shard_map/ppermute | solution.py:453
  3.0 1.8 %tables.1 = (bf16[128,8,2,128]{3,2,1,0:T(2,128)(2,1)S(1)}, s32[1,32]{1,0:T(1,128)S(1)}, bf16[16,256,128]{2,1,0:T(8,128)(2,1)S(1)}, bf16[40,128,128]{2,1,0:T(8,12...) custom-call(bf16[128,8,2,128]{3,2,1,0:T(2,128)(2,1)} %bitcast.15, ...), custom_call_target="tpu_custom_call" | custom-call | flops 65536000 | bytes 2621440 | tf_op jit(solution)/shard_map/tables/pallas_call | solution.py:502
  4.8 0.0 collective-permute-done.1
  4.8 0.8 %product.1.refs_2_ = bf16[2,2,2,128,128]{4,3,2,1,0:T(8,128)(2,1)S(1)} custom-call(bf16[128,8,2,128]{3,2,1,0:T(2,128)(2,1)S(1)} %get-tuple-element.15.refs_0_, bf16[128,8,2,128]{3,2,1,0:T(2,128)(2,1)S(1)} %bitcast.12, bf16[16,256,128]{2,1,0:T(8,128)(2,1)S(1)} %get-tuple-element.16.refs_2_, bf16[40,128,128]{2,1,0:T(8,128)(2,1)S(1)} %get-tuple-element.17.refs_3_.high_ref, ...), custom_call_target="tpu_custom_call" | custom-call | flops 134217728 | bytes 524288 | tf_op jit(solution)/shard_map/product/pallas_call | solution.py:515
  5.6 0.0 collective-permute-done.refs_1_
  5.6 0.9 %levels.1 = f32[128,128]{1,0:T(8,128)S(1)} custom-call(s32[1,32]{1,0:T(1,128)S(1)} %get-tuple-element.14.refs_0_, s32[1,32]{1,0:T(1,128)S(1)} %collective-permute-done.refs_1_, bf16[2,2,2,128,128]{4,3,2,1,0:T(8,128)(2,1)S(1)} %product.1.refs_2_, bf16[40,128,128]{2,1,0:T(8,128)(2,1)S(1)} %get-tuple-element.17.refs_3_.high_ref, ...), custom_call_target="tpu_custom_call" | custom-call | tf_op jit(solution)/shard_map/levels/pallas_call | solution.py:516
  6.5 12.6 %all_to_all.5 = f32[32,4,128]{2,1,0:T(4,128)S(1)} all-to-all(f32[32,4,128]{2,1,0:T(4,128)S(1)} %bitcast.14), channel_id=1, replica_groups=mesh['band'=4,'aperture'=8] {'aperture','band'}, dimensions={0} | all-to-all | bytes 131072 | tf_op jit(solution)/shard_map/all_to_all | solution.py:525
  19.2 1.6 %finish.1 = f32[32,128]{1,0:T(8,128)} custom-call(f32[128,128]{1,0:T(8,128)S(1)} %bitcast.13, bf16[40,128,128]{2,1,0:T(8,128)(2,1)S(1)} %get-tuple-element.17.refs_3_.high_ref, bf16[40,128,128]{2,1,0:T(8,128)(2,1)S(1)} %get-tuple-element.18.refs_4_.low_ref, f32[16,128]{1,0:T(8,128)S(1)} %get-tuple-element.21.cos_ref, f32[16,128]{1,0:T(8,128)S(1)} %get-tuple-element.22.sin_ref), custom_call_target="tpu_custom_call" | custom-call | tf_op jit(solution)/shard_map/finish/pallas_call | solution.py:528
Async XLA Ops:
  0.0 4.8 %collective-permute-start.1 = (bf16[128,2,1024]{2,1,0:T(2,128)(2,1)}, bf16[128,2,1024]{2,1,0:T(2,128)(2,1)S(1)}, u32[]{:S(2)}, u32[]{:S(2)}) collective-permute-start(bf16[128,2,1024]{2,1,0:T(2,128)(2,1)} %param.6), channel_id=1, source_target_pairs={{0,8},{8,0},{16,24},{24,16},{1,9},{9,1},{17,25},{25,17},{2,10},{10... | collective-permute-start | bytes 1572872 | tf_op jit(solution)/shard_map/ppermute | solution.py:457
  0.5 5.1 %collective-permute-start = (s32[1,32]{1,0:T(1,128)}, s32[1,32]{1,0:T(1,128)S(1)}, u32[]{:S(2)}, u32[]{:S(2)}) collective-permute-start(s32[1,32]{1,0:T(1,128)} %bitcast.19), channel_id=1, source_target_pairs={{0,16},{8,24},{16,0},{24,8},{1,17},{9,25},{17,1},{25,9},{2,18},{10... | collective-permute-start | bytes 392 | tf_op jit(solution)/shard_map/ppermute | solution.py:453

commit v8 on v7

--- a/solution.py
+++ b/solution.py
@@ -85,12 +85,11 @@
     return result
 
 
-def build_starts(levels, offsets_ref, fraction_ref, start_ref, edge_ref):
+def build_starts(levels, offsets_ref, fraction_ref, start_ref):
     period = 4 * SHIFT
     lane, row = iota((8, LANES), 1), iota((8, LANES), 0)
     near_tap = lane & (period - 1)
     tap = jnp.where(near_tap < period // 2, -near_tap, period - near_tap).astype(jnp.float32)
-    bands = edge_bands()
     entries = [(n, c, p) for n in range(levels) for c in range(2) for p in range(2)]
     for block in range(0, len(entries), 8):
         here = entries[block : block + 8]
@@ -108,8 +107,6 @@
             one = jnp.broadcast_to(taper[sub : sub + 1, :], (8, LANES))
             one = pltpu.roll(one, (LANES - moved) & (LANES - 1), 1)
             start_ref[block + sub] = pltpu.roll(one, 0, 1, stride=1, stride_axis=0)
-            edge_ref[0, block + sub] = jnp.where(row >= moved, bands[0], 0.0)
-            edge_ref[1, block + sub] = jnp.where(row < moved + 8, bands[-1], 0.0)
 
 
 def build_angles(first_level, count, tilt_ref):
@@ -123,13 +120,19 @@
     return angle
 
 
-def build_matrices(start_ref, edge_ref, band_ref, high_ref, low_ref):
+def build_matrices(offsets_ref, start_ref, band_ref, high_ref, low_ref):
     period = 4 * SHIFT
     for tile, band in enumerate(edge_bands()):
         band_ref[tile] = band
     last = R // 8 - 1
+    row = iota((8, LANES), 0)
     for entry in range(start_ref.shape[0]):
         one = start_ref[entry]
+        moved = offsets_ref[entry // 2 % 2, entry % 2, 0, entry // 4] - SHIFT
+        edges = {
+            0: jnp.where(row >= moved, band_ref[0], 0.0),
+            last: jnp.where(row < moved + 8, band_ref[last], 0.0),
+        }
         turned = [one] + [pltpu.roll(one, begin, 1) for begin in range(8, period, 8)]
         halves = []
         for value in turned:
@@ -139,10 +142,7 @@
             for part, ref in enumerate((high_ref, low_ref)):
                 tiles = []
                 for tile in (begin // 8, begin // 8 + 1):
-                    if tile in (0, last):
-                        keep = edge_ref[tile // last, entry]
-                    else:
-                        keep = band_ref[tile]
+                    keep = edges[tile] if tile in edges else band_ref[tile]
                     tiles.append(halves[tile % len(halves)][part] * keep)
                 ref[entry, begin : begin + 16, :] = jnp.concatenate(tiles, 0).astype(jnp.bfloat16)
 
@@ -178,7 +178,7 @@
 
 def tables_kernel(total_freq, local, inner, fold, echo_hbm, matched_hbm, offsets_hbm, fraction_hbm,
                   tilt_hbm, order_hbm, echo_ref, order_ref, table_ref, high_ref, low_ref,
-                  cos_ref, sin_ref, cos2_ref, sin2_ref, start_ref, edge_ref, band_ref, angle_ref,
+                  cos_ref, sin_ref, cos2_ref, sin2_ref, start_ref, band_ref, angle_ref,
                   matched_ref, offsets_ref, fraction_ref, tilt_ref, sems):
     pairs = (
         (matched_hbm, matched_ref),
@@ -203,10 +203,10 @@
         make_table(total_freq, firsts[side], units[side], matched_ref, table_ref, side * tiles)
     for copy in copies[1:4]:
         copy.wait()
-    build_starts(levels, offsets_ref, fraction_ref, start_ref, edge_ref)
+    build_starts(levels, offsets_ref, fraction_ref, start_ref)
     angle_ref[0:1, :] = build_angles(0, local, tilt_ref)
     angle_ref[1:2, :] = build_angles(local, levels - local, tilt_ref)
-    build_matrices(start_ref, edge_ref, band_ref, high_ref, low_ref)
+    build_matrices(offsets_ref, start_ref, band_ref, high_ref, low_ref)
     phase_tables(0, local, 0, 0, angle_ref[0:1, :], cos_ref, sin_ref)
     place = lax.axis_index("aperture") * bands + band
     tile = bit_reversed(place, (bands * apertures).bit_length() - 1)
@@ -484,7 +484,6 @@
         out_specs=[vmem] * 9,
         scratch_shapes=[
             VMEM((4 * levels, 8, LANES), f32),
-            VMEM((2, 4 * levels, 8, LANES), f32),
             VMEM((R // 8, 8, LANES), f32),
             VMEM((8, LANES), f32),
             VMEM(matched.shape, f32),

time: 20.9 us -> 20.9 us (level)
  no operation moved by 1% of the time
where the time goes in v8:
time: 20.9 us; the launch traced here: 20.7 us
  blocking collectives  12.6 us (60%)
  Pallas kernels  5.08 us (24%)
  starting transfers between devices  3 us (14%)
    all_to_all x1, blocking collectives, body(): lax.all_to_all(sent.reshape(devices, 2 * per, R), ('aperture', 'band'), 0...  12.6 us
    ppermute x1, starting transfers between devices, body(): lax.ppermute(order, 'band', [(n, n ^ apart) for n in range(bands)])  2.51 us
    pallas_call x1, Pallas kernels, body(): tables(*views)  1.8 us
    pallas_call x1, Pallas kernels, body(): pl.pallas_call(functools.partial(final_kernel, local, rest, fold), out_sh...  1.57 us
    pallas_call x1, Pallas kernels, body(): pl.pallas_call(functools.partial(local_kernel, local, fold), out_shape=sh...  0.91 us
    pallas_call x1, Pallas kernels, body(): prof = product(*echoes, table, high, low, cos_1, sin_1)  0.8 us
    ppermute x1, starting transfers between devices, body(): echo_parts.append(lax.ppermute(raw_echoes, 'band', pairs))  0.49 us
  transfers between devices with their start and end apart: 2, of which 0 were waited for; matrix products, arithmetic and copies ran while one was open for 0% of the time, Pallas kernels for 13%

profile of v8, /device:TPU:0, one launch (start us, length us, event | category | flops | bytes accessed | tf_op | source)
XLA Modules:
  0.0 20.7 jit_solution(12728038989668031188)
XLA Ops:
  0.0 0.5 %collective-permute-start.1 = (bf16[128,2,1024]{2,1,0:T(2,128)(2,1)}, bf16[128,2,1024]{2,1,0:T(2,128)(2,1)S(1)}, u32[]{:S(2)}, u32[]{:S(2)}) collective-permute-start(bf16[128,2,1024]{2,1,0:T(2,128)(2,1)} %param.6), channel_id=1, source_target_pairs={{0,8},{8,0},{16,24},{24,16},{1,9},{9,1},{17,25},{25,17},{2,10},{10... | collective-permute-start | bytes 1572872 | tf_op jit(solution)/shard_map/ppermute | solution.py:457
  0.5 2.5 %collective-permute-start = (s32[1,32]{1,0:T(1,128)}, s32[1,32]{1,0:T(1,128)S(1)}, u32[]{:S(2)}, u32[]{:S(2)}) collective-permute-start(s32[1,32]{1,0:T(1,128)} %bitcast.19), channel_id=1, source_target_pairs={{0,16},{8,24},{16,0},{24,8},{1,17},{9,25},{17,1},{25,9},{2,18},{10... | collective-permute-start | bytes 392 | tf_op jit(solution)/shard_map/ppermute | solution.py:453
  3.0 1.8 %tables.1 = (bf16[128,8,2,128]{3,2,1,0:T(2,128)(2,1)S(1)}, s32[1,32]{1,0:T(1,128)S(1)}, bf16[16,256,128]{2,1,0:T(8,128)(2,1)S(1)}, bf16[40,128,128]{2,1,0:T(8,12...) custom-call(bf16[128,8,2,128]{3,2,1,0:T(2,128)(2,1)} %bitcast.15, ...), custom_call_target="tpu_custom_call" | custom-call | flops 65536000 | bytes 2621440 | tf_op jit(solution)/shard_map/tables/pallas_call | solution.py:501
  4.8 0.0 collective-permute-done.1
  4.8 0.8 %product.1.refs_2_ = bf16[2,2,2,128,128]{4,3,2,1,0:T(8,128)(2,1)S(1)} custom-call(bf16[128,8,2,128]{3,2,1,0:T(2,128)(2,1)S(1)} %get-tuple-element.15.refs_0_, bf16[128,8,2,128]{3,2,1,0:T(2,128)(2,1)S(1)} %bitcast.12, bf16[16,256,128]{2,1,0:T(8,128)(2,1)S(1)} %get-tuple-element.16.refs_2_, bf16[40,128,128]{2,1,0:T(8,128)(2,1)S(1)} %get-tuple-element.17.refs_3_.high_ref, ...), custom_call_target="tpu_custom_call" | custom-call | flops 134217728 | bytes 524288 | tf_op jit(solution)/shard_map/product/pallas_call | solution.py:514
  5.6 0.0 collective-permute-done.refs_1_
  5.6 0.9 %levels.1 = f32[128,128]{1,0:T(8,128)S(1)} custom-call(s32[1,32]{1,0:T(1,128)S(1)} %get-tuple-element.14.refs_0_, s32[1,32]{1,0:T(1,128)S(1)} %collective-permute-done.refs_1_, bf16[2,2,2,128,128]{4,3,2,1,0:T(8,128)(2,1)S(1)} %product.1.refs_2_, bf16[40,128,128]{2,1,0:T(8,128)(2,1)S(1)} %get-tuple-element.17.refs_3_.high_ref, ...), custom_call_target="tpu_custom_call" | custom-call | tf_op jit(solution)/shard_map/levels/pallas_call | solution.py:515
  6.5 12.6 %all_to_all.5 = f32[32,4,128]{2,1,0:T(4,128)S(1)} all-to-all(f32[32,4,128]{2,1,0:T(4,128)S(1)} %bitcast.14), channel_id=1, replica_groups=mesh['band'=4,'aperture'=8] {'aperture','band'}, dimensions={0} | all-to-all | bytes 131072 | tf_op jit(solution)/shard_map/all_to_all | solution.py:524
  19.2 1.6 %finish.1 = f32[32,128]{1,0:T(8,128)} custom-call(f32[128,128]{1,0:T(8,128)S(1)} %bitcast.13, bf16[40,128,128]{2,1,0:T(8,128)(2,1)S(1)} %get-tuple-element.17.refs_3_.high_ref, bf16[40,128,128]{2,1,0:T(8,128)(2,1)S(1)} %get-tuple-element.18.refs_4_.low_ref, f32[16,128]{1,0:T(8,128)S(1)} %get-tuple-element.21.cos_ref, f32[16,128]{1,0:T(8,128)S(1)} %get-tuple-element.22.sin_ref), custom_call_target="tpu_custom_call" | custom-call | tf_op jit(solution)/shard_map/finish/pallas_call | solution.py:527
Async XLA Ops:
  0.0 4.8 %collective-permute-start.1 = (bf16[128,2,1024]{2,1,0:T(2,128)(2,1)}, bf16[128,2,1024]{2,1,0:T(2,128)(2,1)S(1)}, u32[]{:S(2)}, u32[]{:S(2)}) collective-permute-start(bf16[128,2,1024]{2,1,0:T(2,128)(2,1)} %param.6), channel_id=1, source_target_pairs={{0,8},{8,0},{16,24},{24,16},{1,9},{9,1},{17,25},{25,17},{2,10},{10... | collective-permute-start | bytes 1572872 | tf_op jit(solution)/shard_map/ppermute | solution.py:457
  0.5 5.1 %collective-permute-start = (s32[1,32]{1,0:T(1,128)}, s32[1,32]{1,0:T(1,128)S(1)}, u32[]{:S(2)}, u32[]{:S(2)}) collective-permute-start(s32[1,32]{1,0:T(1,128)} %bitcast.19), channel_id=1, source_target_pairs={{0,16},{8,24},{16,0},{24,8},{1,17},{9,25},{17,1},{25,9},{2,18},{10... | collective-permute-start | bytes 392 | tf_op jit(solution)/shard_map/ppermute | solution.py:453
